TPU v7x, 32 devices: a whole 2x2x4 slice. The times are simulated.
32 devices in a mesh: dp: 2 (over x), tensor: 4 (over y, core), latent: 4 (over z).
Axes of the slice: x: 2, y: 2, z: 4, core: 2. Of those that a mesh axis runs over, the one named last changes fastest.
Arguments:
- residual: bfloat16 [256, 4608], P('dp', ('tensor', 'latent')), may hold values from -6 to 6
- segments: int32 [2, 128], P('dp'), may hold values from 0 to 3, never falling along the last dimension, each value on 1 to 64 neighbouring positions
- row_perm: int32 [256], P('dp'), may hold values from 0 to 255, as said below
- pre_gain: float32 [4608], replicated, may hold values from 0.25 to 1.75
- post_gain: float32 [4608], replicated, may hold values from 0.25 to 1.75
- w_query: bfloat16 [4608, 4096], P(None, ('tensor', 'latent')), may hold values from -0.70710678 to 0.70710678
- w_key: bfloat16 [4608, 2048], P(None, ('tensor', 'latent')), may hold values from -0.09375 to 0.09375
- w_value: bfloat16 [4608, 2048], P(None, ('tensor', 'latent')), may hold values from -0.09375 to 0.09375
- w_out: bfloat16 [4096, 4608], P(('tensor', 'latent')), may hold values from -0.09375 to 0.09375
- sae_weight: bfloat16 [4608, 16384], P('dp', ('tensor', 'latent')), may hold values from -0.09375 to 0.09375
- enc_bias: float32 [16384], P(('tensor', 'latent')), may hold values from -3 to 3
- thresholds: float32 [16384], P(('tensor', 'latent')), may hold values from 0.2 to 1.2
- dec_bias: float32 [4608], replicated, may hold values from -3 to 3
Outputs:
- weight_grad: bfloat16 [4608, 16384], P('dp', ('tensor', 'latent'))
- bias_grad: float32 [16384], P(('tensor', 'latent'))
- codes: bfloat16 [256, 16384], P('dp', ('tensor', 'latent'))
Inputs may be any that keep to these rules, and one draw needn't show every extreme that they name: `segments`: segment numbers never fall along a row. row_perm is a permutation. Within the rows 128 g to 128 (g + 1) - 1, the 64 rows starting at 128 g + s * 64 hold only indices from 128 s to 128 (s + 1) - 1.
All inputs are finite; a program needn't handle non-finite values.
Results may differ from a plain program's by a relative error of at most 0.03.
Values may be sent and summed in bfloat16 or wider, within the bound.
No kernel may reach another device: no remote copies, remote signals or barrier semaphores. Data moves between devices by JAX's collectives and lax.ppermute only.
A program may use at most 128 MiB of HBM per device.

v0:
```python
import math

import jax
import jax.numpy as jnp
from jax import lax
from jax.experimental import pallas as pl
from jax.experimental.pallas import tpu as pltpu
from jax.sharding import PartitionSpec as P


D = 4608
HEADS = 32
HEAD = 128

epsilon = 1e-06
softcap = 50.0
ramp_width = 0.05
rotary_base = 10000.0
BF = jnp.bfloat16
F32 = jnp.float32
VMEM_LIMIT = 28 * 1024 * 1024


def swap(values, axis, mask):
    size = lax.axis_size(axis)
    return lax.ppermute(values, axis, [(i, i ^ mask) for i in range(size)])


def plane_stages():
    tensor, latent = lax.axis_size("tensor"), lax.axis_size("latent")
    cores = 2 if tensor % 2 == 0 else 1
    stages = []
    if cores > 1:
        stages.append(("tensor", [1]))
    if tensor > cores:
        stages.append(("tensor", [k * cores for k in range(1, tensor // cores)]))
    if latent > 1:
        stages.append(("latent", list(range(1, latent))))
    return stages


def plane_index():
    tensor, latent = lax.axis_size("tensor"), lax.axis_size("latent")
    cores = 2 if tensor % 2 == 0 else 1
    t, z = lax.axis_index("tensor"), lax.axis_index("latent")
    return ((t % cores) * (tensor // cores) + t // cores) * latent + z


def gather_blocks(block, gate=None):
    stages = plane_stages()
    for place in reversed(range(len(stages))):
        axis, masks = stages[place]
        pieces = [block] + [swap(block, axis, m) for m in masks]
        if place == 1 and gate is not None:
            pieces = gate(pieces)
        block = jnp.concatenate(pieces, axis=0)
    return block


def add_arrived(kept, sent, stage):
    axis, masks = stage
    total = kept
    for m, part in zip(masks, sent):
        total = total + swap(part, axis, m).astype(F32)
    return total


def scatter_sum(partial, done=0):
    for place, stage in enumerate(plane_stages()):
        if place < done:
            continue
        parts = partial.reshape((len(stage[1]) + 1, -1) + partial.shape[1:])
        sent = [parts[k + 1].astype(BF) for k in range(len(stage[1]))]
        partial = add_arrived(parts[0].astype(F32), sent, stage)
    return partial


def rotary_tables(positions):
    half_width = HEAD // 2
    frequency = rotary_base ** (-2.0 * jnp.arange(half_width, dtype=F32) / HEAD)
    angles = positions[:, None] * frequency
    cosine, sine = jnp.cos(angles), jnp.sin(angles)
    return jnp.concatenate([cosine, cosine], 1), jnp.concatenate([-sine, sine], 1)


def doc_masks(segment_ids):
    same_doc = segment_ids[..., :, None] == segment_ids[..., None, :]
    indices = jnp.arange(segment_ids.shape[-1], dtype=jnp.int32)
    earlier = indices[None, :] < indices[:, None]
    positions = jnp.sum((same_doc & earlier).astype(F32), axis=-1)
    attend_mask = (same_doc & (indices[None, :] <= indices[:, None])).astype(F32)
    return (positions, attend_mask)


def hold_on_chip(values, after):
    def body(source, _, held, sem):
        copy = pltpu.make_async_copy(source, held, sem)
        copy.start()
        copy.wait()

    return pl.pallas_call(
        body,
        out_shape=pltpu.VMEM(values.shape, values.dtype),
        in_specs=[pl.BlockSpec(memory_space=pltpu.HBM), pl.BlockSpec(memory_space=pl.ANY)],
        out_specs=pl.BlockSpec(memory_space=pltpu.VMEM),
        scratch_shapes=[pltpu.SemaphoreType.DMA],
        compiler_params=pltpu.CompilerParams(vmem_limit_bytes=1024 * 1024),
        cost_estimate=pl.CostEstimate(
            flops=0, bytes_accessed=2 * values.size, transcendentals=0
        ),
    )(values, after)


def attention_body(
    sizes,
    feature_table,
    token_table,
    blocks,
    gain,
    cosine,
    sine,
    mask,
    pick,
    w_query,
    w_key,
    w_value,
    w_out,
    kept,
    sent,
    own,
    weight,
    weight_out,
    stream,
    normed,
    heads,
    sems,
):
    plane, columns, length, rows, query_heads, key_heads = sizes
    query_width, key_width = query_heads * HEAD, key_heads * HEAD
    starts = [0, query_width, query_width + key_width]
    copies = [
        pltpu.make_async_copy(src, weight.at[:, pl.ds(start, src.shape[1])], sems.at[k])
        for k, (src, start) in enumerate(zip((w_query, w_key, w_value), starts))
    ]
    copies.append(pltpu.make_async_copy(w_out, weight_out, sems.at[3]))
    for copy in copies:
        copy.start()
    squares = jnp.zeros((1, length), F32)
    for j in range(plane):
        block = blocks[feature_table[j]]
        stream[j * columns : (j + 1) * columns] = block
        wide = block.astype(F32)
        squares = squares + jnp.sum(wide * wide, axis=0, keepdims=True)
    scale = lax.rsqrt(squares / (plane * columns) + epsilon)
    for j in range(plane):
        part = slice(j * columns, (j + 1) * columns)
        normed[part] = (stream[part].astype(F32) * scale * gain[part]).astype(BF)
    own[...] = lax.dot_general(
        pick[...], stream[...], (((1,), (1,)), ((), ())), preferred_element_type=F32
    )
    for copy in copies[:3]:
        copy.wait()
    projected = lax.dot_general(
        normed[...], weight[...], (((0,), (0,)), ((), ())), preferred_element_type=F32
    )

    def turned(start):
        field = projected[:, start : start + HEAD]
        return (field * cosine[...] + pltpu.roll(field, HEAD // 2, 1) * sine[...]).astype(BF)

    for j in range(query_heads):
        group = j // (query_heads // key_heads)
        query = turned(j * HEAD)
        key = turned(starts[1] + group * HEAD)
        value = projected[:, starts[2] + group * HEAD : starts[2] + (group + 1) * HEAD].astype(BF)
        logits = lax.dot_general(
            query, key, (((1,), (1,)), ((), ())), preferred_element_type=F32
        ) * (D / HEADS) ** (-0.5)
        logits = softcap * jnp.tanh(logits / softcap)
        weighted = jnp.exp(logits) * mask[...]
        probs = (weighted / jnp.sum(weighted, axis=-1, keepdims=True)).astype(BF)
        heads[:, j * HEAD : (j + 1) * HEAD] = jnp.dot(probs, value, preferred_element_type=F32)
    moved = [heads[pl.ds(pl.multiple_of(token_table[k] * rows, 8), rows)] for k in range(plane)]
    moved = jnp.concatenate(moved, 0).astype(BF)
    copies[3].wait()
    middle = length // 2
    step = 512
    for start in range(0, weight_out.shape[1], step):
        part = slice(start, min(start + step, weight_out.shape[1]))
        product = jnp.dot(moved, weight_out[:, part], preferred_element_type=F32)
        kept[:, part] = product[:middle]
        sent[:, part] = product[middle:].astype(BF)


def attention_tables(segments, pre_gain, me, rows):
    length = segments.shape[0]
    positions, mask = doc_masks(segments)
    cosine, sine = rotary_tables(positions)
    gain = jnp.broadcast_to(pre_gain[:, None], (pre_gain.shape[0], length))
    token = jnp.arange(length, dtype=jnp.int32)[None, :]
    pick = (token == me * rows + jnp.arange(rows, dtype=jnp.int32)[:, None]).astype(BF)
    return gain, cosine, sine, mask, pick


def attention(blocks, feature_table, token_table, tables, weights):
    plane, columns, length = blocks.shape
    rows = length // plane
    features = plane * columns
    w_query, w_key, w_value, w_out = weights
    sizes = (plane, columns, length, rows, w_query.shape[1] // HEAD, w_key.shape[1] // HEAD)
    vmem = pl.BlockSpec(memory_space=pltpu.VMEM)
    smem = pl.BlockSpec(memory_space=pltpu.SMEM)
    anywhere = pl.BlockSpec(memory_space=pl.ANY)
    width = w_query.shape[1] + w_key.shape[1] + w_value.shape[1]
    total = w_out.shape[1]
    return pl.pallas_call(
        lambda *refs: attention_body(sizes, *refs),
        out_shape=(
            jax.ShapeDtypeStruct((length // 2, total), F32),
            jax.ShapeDtypeStruct((length // 2, total), BF),
            jax.ShapeDtypeStruct((rows, features), F32),
        ),
        in_specs=[smem] * 2 + [vmem] * 6 + [anywhere] * 4,
        out_specs=(vmem,) * 3,
        scratch_shapes=[
            pltpu.VMEM((features, width), BF),
            pltpu.VMEM(w_out.shape, BF),
            pltpu.VMEM((features, length), BF),
            pltpu.VMEM((features, length), BF),
            pltpu.VMEM((length, w_query.shape[1]), F32),
            pltpu.SemaphoreType.DMA((4,)),
        ],
        compiler_params=pltpu.CompilerParams(vmem_limit_bytes=VMEM_LIMIT),
        cost_estimate=pl.CostEstimate(
            flops=2 * length * (features * width + w_query.shape[1] * total),
            bytes_accessed=2 * (features * width + w_out.size),
            transcendentals=0,
        ),
    )(
        feature_table,
        token_table,
        blocks,
        *tables,
        w_query,
        w_key,
        w_value,
        w_out,
    )


def local(
    residual,
    segments,
    row_perm,
    pre_gain,
    post_gain,
    w_query,
    w_key,
    w_value,
    w_out,
    sae_weight,
    enc_bias,
    thresholds,
    dec_bias,
):
    groups = lax.axis_size("dp")
    tensor, latent = lax.axis_size("tensor"), lax.axis_size("latent")
    plane = tensor * latent
    length = residual.shape[0]
    rows = length // plane
    half = sae_weight.shape[0]
    me = plane_index()
    mine = lax.axis_index("dp")
    cores = 2 if tensor % 2 == 0 else 1
    contract_last = (((1,), (1,)), ((), ()))

    tables = list(attention_tables(segments[0], pre_gain, me, rows))
    flat = jnp.arange(plane, dtype=jnp.int32)
    t_of, z_of = flat // latent, flat % latent
    number = ((t_of % cores) * (tensor // cores) + t_of // cores) * latent + z_of
    tables += [number ^ me, flat ^ me]

    def gate(pieces):
        held = lax.optimization_barrier(pieces + tables)
        tables[:] = held[len(pieces) :]
        return held[: len(pieces)]

    blocks = gather_blocks(residual.T[None], gate)
    kept_rows, sent_rows, own = attention(
        blocks, tables[-2], tables[-1], tables[:-2], (w_query, w_key, w_value, w_out)
    )
    attn_out = add_arrived(kept_rows, [sent_rows], plane_stages()[0])
    attn_out = scatter_sum(attn_out, 1)
    scale = lax.rsqrt(jnp.mean(attn_out * attn_out, axis=-1, keepdims=True) + epsilon)
    hidden = (own + attn_out * scale * post_gain).astype(BF)
    pieces = hidden.reshape(rows, groups, half).transpose(1, 0, 2)

    def piece(k):
        return lax.dynamic_index_in_dim(pieces, mine ^ k, 0, keepdims=False)

    others = jnp.stack([swap(piece(k), "dp", k) for k in range(1, groups)], 0)

    def spread(stack):
        count = stack.shape[0]
        if count == 1:
            return gather_blocks(stack[0])
        out = gather_blocks(stack.transpose(1, 0, 2).reshape(rows, count * half))
        out = out.reshape(length, count, half).transpose(1, 0, 2)
        return out.reshape(count * length, half)

    weights = {}

    def keep_weight(name):
        def gate(pieces):
            held = hold_on_chip(sae_weight, pieces[0])
            held = lax.optimization_barrier(pieces + [held])
            weights[name] = held[-1]
            return held[:-1]

        return gate

    sae = [gather_blocks(piece(0), keep_weight("pre_a")), spread(others)]

    def partial_pair(values, label):
        out = jnp.dot(values, weights.get(label, sae_weight), preferred_element_type=F32)
        return lax.optimization_barrier((out, out.astype(BF)))

    def across(chunks, label):
        (first_part, first_sent), (rest, rest_sent) = [
            partial_pair(c, f"{label}_{k}") for k, c in zip("ab", chunks)
        ]
        if groups == 2:
            got_rest = swap(first_sent, "dp", 1)
            got_first = swap(rest_sent, "dp", 1)
            return (first_part, got_first), (rest, got_rest)
        total = jnp.concatenate([first_part, rest], 0)
        masks = [1 << k for k in range(groups.bit_length() - 1)]
        for m in reversed(masks):
            keep, send = jnp.split(total, 2, axis=0)
            total = keep + swap(send.astype(BF), "dp", m).astype(F32)
        for m in masks:
            total = jnp.concatenate([total, swap(total, "dp", m)], 0)
        none = jnp.zeros((), BF)
        return (total[:length], none), (total[length:], none)

    def opened(own_part, arrived):
        pre = own_part + arrived.astype(F32) + enc_bias
        gate = jax.nn.sigmoid((pre - thresholds) / ramp_width)
        slope = gate + pre * gate * (1.0 - gate) / ramp_width
        return lax.optimization_barrier(((pre * gate).astype(BF), slope))

    codes, slopes = [None, None], [None, None]
    (first_part, first_arrived), (rest, rest_arrived) = across(sae, "pre")
    codes[1], slopes[1] = opened(rest, rest_arrived)
    _, first_arrived = lax.optimization_barrier((codes[1], first_arrived))
    codes[0], slopes[0] = opened(first_part, first_arrived)

    half_bias = lax.dynamic_slice(dec_bias, (mine * half,), (half,))

    def rebuild(chunk, count, after):
        part = lax.dot_general(codes[chunk], sae_weight, contract_last, preferred_element_type=F32)
        if count > 1:
            part = part.reshape(count, plane, rows, half).transpose(1, 0, 2, 3)
            part = part.reshape(plane * count * rows, half)
        total = scatter_sum(part)
        if count > 1:
            held = sae[chunk].reshape(count, plane, rows, half)[:, 0].reshape(count * rows, half)
        else:
            held = sae[chunk][:rows]
        if after is not None:
            total, _ = lax.optimization_barrier((total, after))
        error = (total + half_bias - held.astype(F32)).astype(BF)
        error = lax.optimization_barrier(error)
        out = gather_blocks(error, keep_weight("lat_b") if chunk else None)
        if count > 1:
            out = out.reshape(plane, count, rows, half).transpose(1, 0, 2, 3)
            out = out.reshape(count * length, half)
        return out, error

    error = [None, None]
    error[1], after = rebuild(1, groups - 1, None)
    error[0], _ = rebuild(0, 1, after)
    grad_scale = 1.0 / math.sqrt(length * groups)
    (first_part, first_arrived), (rest, rest_arrived) = across(error, "lat")
    grad_pre = [None, None]
    grad_pre[0] = ((first_part + first_arrived.astype(F32)) * slopes[0]).astype(BF)
    _, rest_arrived = lax.optimization_barrier((grad_pre[0], rest_arrived))
    grad_pre[1] = ((rest + rest_arrived.astype(F32)) * slopes[1]).astype(BF)
    total, hidden_t = early_gradient(error, codes, sae)
    weight_grad = late_gradient(total, hidden_t, grad_pre, grad_scale)
    bias_grad = grad_scale * sum(jnp.sum(g.astype(F32), axis=0) for g in grad_pre)

    place = row_perm ^ ((mine * plane + me) * rows)
    chosen = (place[:, None] == jnp.arange(length * groups, dtype=jnp.int32)[None, :]).astype(BF)
    out_codes = jnp.dot(chosen, jnp.concatenate(codes, 0), preferred_element_type=F32).astype(BF)
    return (weight_grad, bias_grad, out_codes)


def early_gradient(error, codes, hidden):
    tokens = sum(e.shape[0] for e in error)
    half, latents = error[0].shape[1], codes[0].shape[1]
    first = error[0].shape[0]

    def body(error_a, error_b, codes_a, codes_b, hidden_a, hidden_b, total, turned, left, right):
        left[:, :first] = error_a[...].T
        left[:, first:] = error_b[...].T
        right[:first] = codes_a[...]
        right[first:] = codes_b[...]
        total[...] = jnp.dot(left[...], right[...], preferred_element_type=F32)
        turned[:, :first] = hidden_a[...].T
        turned[:, first:] = hidden_b[...].T

    vmem = pl.BlockSpec(memory_space=pltpu.VMEM)
    return pl.pallas_call(
        body,
        out_shape=(pltpu.VMEM((half, latents), F32), pltpu.VMEM((half, tokens), BF)),
        in_specs=[vmem] * 6,
        out_specs=(vmem,) * 2,
        scratch_shapes=[pltpu.VMEM((half, tokens), BF), pltpu.VMEM((tokens, latents), BF)],
        compiler_params=pltpu.CompilerParams(vmem_limit_bytes=VMEM_LIMIT),
        cost_estimate=pl.CostEstimate(
            flops=2 * half * latents * tokens, bytes_accessed=4 * half * latents, transcendentals=0
        ),
    )(*error, *codes, *hidden)


def late_gradient(total, turned, grad_pre, grad_scale):
    half, latents = total.shape
    tile = max(t for t in range(16, 257, 16) if half % t == 0)
    first = grad_pre[0].shape[0]

    steps = half // tile

    def body(total, turned, grad_a, grad_b, out, right, ready, sems):
        right[:first] = grad_a[...]
        right[first:] = grad_b[...]

        def put(i):
            part = pl.ds(i * tile, tile)
            return pltpu.make_async_copy(ready.at[part], out.at[part], sems.at[i])

        for i in range(steps):
            part = pl.ds(i * tile, tile)
            product = jnp.dot(turned[part], right[...], preferred_element_type=F32)
            ready[part] = (grad_scale * (total[part] + product)).astype(BF)
            put(i).start()
        for i in range(steps):
            put(i).wait()

    vmem = pl.BlockSpec(memory_space=pltpu.VMEM)
    return pl.pallas_call(
        body,
        out_shape=jax.ShapeDtypeStruct((half, latents), BF),
        in_specs=[vmem] * 4,
        out_specs=pl.BlockSpec(memory_space=pltpu.HBM),
        scratch_shapes=[
            pltpu.VMEM((turned.shape[1], latents), BF),
            pltpu.VMEM((half, latents), BF),
            pltpu.SemaphoreType.DMA((steps,)),
        ],
        compiler_params=pltpu.CompilerParams(vmem_limit_bytes=VMEM_LIMIT),
        cost_estimate=pl.CostEstimate(
            flops=2 * half * latents * turned.shape[1],
            bytes_accessed=6 * half * latents,
            transcendentals=0,
        ),
    )(total, turned, *grad_pre)


def solution(mesh):
    return jax.shard_map(
        local,
        mesh=mesh,
        in_specs=(
            P("dp", ("tensor", "latent")),
            P("dp", None),
            P("dp"),
            P(),
            P(),
            P(None, ("tensor", "latent")),
            P(None, ("tensor", "latent")),
            P(None, ("tensor", "latent")),
            P(("tensor", "latent"), None),
            P("dp", ("tensor", "latent")),
            P(("tensor", "latent")),
            P(("tensor", "latent")),
            P(),
        ),
        out_specs=(
            P("dp", ("tensor", "latent")),
            P(("tensor", "latent")),
            P("dp", ("tensor", "latent")),
        ),
        check_vma=False,
    )
```

profile of v0, /device:TPU:0, one launch (start us, length us, event | category | flops | bytes accessed | tf_op | source)
XLA Modules:
  0.0 141.0 jit_solution(13190641544769883875)
XLA Ops:
  0.6 5.1 %collective-permute-start.2 = (bf16[1,288,128]{2,1,0:T(8,128)(2,1)}, bf16[1,288,128]{2,1,0:T(8,128)(2,1)S(1)}, u32[]{:S(2)}, u32[]{:S(2)}) collective-permute-start(bf16[1,288,128]{2,1,0:T(8,128)(2,1)} %bitcast.24), channel_id=1, source_target_pairs={{0,3},{1,2},{2,1},{3,0},{4,7},{5,6},{6,5},{7,4},{8,11},{9,10},{10,... | collective-permute-start | bytes 221192 | tf_op jit(solution)/shard_map/ppermute | solution.py:26
  8.7 3.5 %collective-permute-done.1 = bf16[1,288,128]{2,1,0:T(8,128)(2,1)S(1)} collective-permute-done((bf16[1,288,128]{2,1,0:T(8,128)(2,1)}, bf16[1,288,128]{2,1,0:T(8,128)(2,1)S(1)}, u32[]{:S(2)}, u32[]{:S(2)}) %collective-permute-start.1) | collective-permute-done | bytes 73760 | tf_op jit(solution)/shard_map/ppermute | solution.py:26
  15.6 6.0 %collective-permute-done.3 = bf16[4,288,128]{2,1,0:T(8,128)(2,1)S(1)} collective-permute-done((bf16[4,288,128]{2,1,0:T(8,128)(2,1)S(1)}, bf16[4,288,128]{2,1,0:T(8,128)(2,1)S(1)}, u32[]{:S(2)}, u32[]{:S(2)}) %collective-permute-start.3) | collective-permute-done | bytes 294944 | tf_op jit(solution)/shard_map/ppermute | solution.py:26
  23.2 2.0 %collective-permute-done.4 = bf16[8,288,128]{2,1,0:T(8,128)(2,1)S(1)} collective-permute-done((bf16[8,288,128]{2,1,0:T(8,128)(2,1)S(1)}, bf16[8,288,128]{2,1,0:T(8,128)(2,1)S(1)}, u32[]{:S(2)}, u32[]{:S(2)}) %collective-permute-start.4) | collective-permute-done | bytes 589856 | tf_op jit(solution)/shard_map/ppermute | solution.py:26
  25.4 3.9 %shard_map.148 = (f32[64,4608]{1,0:T(8,128)S(1)}, bf16[64,4608]{1,0:T(8,128)(2,1)S(1)}, f32[8,4608]{1,0:T(8,128)S(1)}) custom-call(s32[16]{0:T(128)S(1)} %get-tuple-element.38.refs_0_, s32[16]{0:T(128)S(1)} %get-tuple-element.39.refs_1_, bf16[16,288,128]{2,1,0:T(8,128)(2,1)S(1)} %pad_maximum_fusion.refs_2_, f32[4608,128]{1,0:T(8,128)S(1)} %broadcast_in_dim.5.refs_3_, ...), custom_call_target="tpu_custom_call" | custom-call | flops 905969664 | bytes 7077888 | tf_op jit(solution)/shard_map/pallas_call | solution.py:216
  29.5 1.9 %collective-permute-done.5 = bf16[64,4608]{1,0:T(8,128)(2,1)S(1)} collective-permute-done((bf16[64,4608]{1,0:T(8,128)(2,1)S(1)}, bf16[64,4608]{1,0:T(8,128)(2,1)S(1)}, u32[]{:S(2)}, u32[]{:S(2)}) %collective-permute-start.5) | collective-permute-done | bytes 589856 | tf_op jit(solution)/shard_map/ppermute | solution.py:26
  31.5 1.8 %collective-permute-start.6 = (bf16[32,4608]{1,0:T(8,128)(2,1)S(1)}, bf16[32,4608]{1,0:T(8,128)(2,1)S(1)}, u32[]{:S(2)}, u32[]{:S(2)}) collective-permute-start(bf16[32,4608]{1,0:T(8,128)(2,1)S(1)} %slice.188), channel_id=1, source_target_pairs={{0,8},{4,12},{8,0},{12,4},{1,9},{5,13},{9,1},{13,5},{2,10},{6,14},... | collective-permute-start | bytes 884744 | tf_op jit(solution)/shard_map/ppermute | solution.py:26
  33.3 7.4 %collective-permute-done.6 = bf16[32,4608]{1,0:T(8,128)(2,1)S(1)} collective-permute-done((bf16[32,4608]{1,0:T(8,128)(2,1)S(1)}, bf16[32,4608]{1,0:T(8,128)(2,1)S(1)}, u32[]{:S(2)}, u32[]{:S(2)}) %collective-permute-start.6) | collective-permute-done | bytes 294944 | tf_op jit(solution)/shard_map/ppermute | solution.py:26
  44.3 1.9 %collective-permute-done.7 = bf16[8,4608]{1,0:T(8,128)(2,1)S(1)} collective-permute-done((bf16[8,4608]{1,0:T(8,128)(2,1)S(1)}, bf16[8,4608]{1,0:T(8,128)(2,1)S(1)}, u32[]{:S(2)}, u32[]{:S(2)}) %collective-permute-start.7) | collective-permute-done | bytes 73760 | tf_op jit(solution)/shard_map/ppermute | solution.py:26
  47.4 3.0 %collective-permute-done.8 = bf16[8,4608]{1,0:T(8,128)(2,1)S(1)} collective-permute-done((bf16[8,4608]{1,0:T(8,128)(2,1)S(1)}, bf16[8,4608]{1,0:T(8,128)(2,1)S(1)}, u32[]{:S(2)}, u32[]{:S(2)}) %collective-permute-start.8) | collective-permute-done | bytes 73760 | tf_op jit(solution)/shard_map/ppermute | solution.py:26
  50.7 1.9 %collective-permute-start.12 = (bf16[8,2304]{1,0:T(8,128)(2,1)S(1)}, bf16[8,2304]{1,0:T(8,128)(2,1)S(1)}, u32[]{:S(2)}, u32[]{:S(2)}) collective-permute-start(bf16[8,2304]{1,0:T(8,128)(2,1)S(1)} %get-tuple-element.101), channel_id=1, source_target_pairs={{0,3},{1,2},{2,1},{3,0},{4,7},{5,6},{6,5},{7,4},{8,11},{9,10},{10,... | collective-permute-start | bytes 110600 | tf_op jit(solution)/shard_map/ppermute | solution.py:26
  52.6 2.5 %collective-permute-start.10 = (bf16[8,2304]{1,0:T(8,128)(2,1)S(1)}, bf16[8,2304]{1,0:T(8,128)(2,1)S(1)}, u32[]{:S(2)}, u32[]{:S(2)}) collective-permute-start(bf16[8,2304]{1,0:T(8,128)(2,1)S(1)} %get-tuple-element.101), channel_id=1, source_target_pairs={{0,1},{1,0},{2,3},{3,2},{4,5},{5,4},{6,7},{7,6},{8,9},{9,8},{10,11... | collective-permute-start | bytes 110600 | tf_op jit(solution)/shard_map/ppermute | solution.py:26
  57.5 1.7 %collective-permute-start.13 = (bf16[32,2304]{1,0:T(8,128)(2,1)S(1)}, bf16[32,2304]{1,0:T(8,128)(2,1)S(1)}, u32[]{:S(2)}, u32[]{:S(2)}) collective-permute-start(bf16[32,2304]{1,0:T(8,128)(2,1)S(1)} %pad_maximum_fusion.5._), channel_id=1, source_target_pairs={{0,8},{4,12},{8,0},{12,4},{1,9},{5,13},{9,1},{13,5},{2,10},{6,14},... | collective-permute-start | bytes 442376 | tf_op jit(solution)/shard_map/ppermute | solution.py:26
  59.2 2.0 %collective-permute-start.18 = (bf16[8,2304]{1,0:T(8,128)(2,1)S(1)}, bf16[8,2304]{1,0:T(8,128)(2,1)S(1)}, u32[]{:S(2)}, u32[]{:S(2)}) collective-permute-start(bf16[8,2304]{1,0:T(8,128)(2,1)S(1)} %collective-permute-done.15), channel_id=1, source_target_pairs={{0,3},{1,2},{2,1},{3,0},{4,7},{5,6},{6,5},{7,4},{8,11},{9,10},{10,... | collective-permute-start | bytes 110600 | tf_op jit(solution)/shard_map/ppermute | solution.py:26
  63.6 2.3 %copy-done = bf16[2304,1024]{1,0:T(8,128)(2,1)S(1)} copy-done((bf16[2304,1024]{1,0:T(8,128)(2,1)S(1)}, bf16[2304,1024]{1,0:T(8,128)(2,1)}, u32[]{:S(2)}) %copy-start) | copy-done | bytes 4718616
  68.2 3.5 %collective-permute-done.19 = bf16[32,2304]{1,0:T(8,128)(2,1)S(1)} collective-permute-done((bf16[32,2304]{1,0:T(8,128)(2,1)S(1)}, bf16[32,2304]{1,0:T(8,128)(2,1)S(1)}, u32[]{:S(2)}, u32[]{:S(2)}) %collective-permute-start.19) | collective-permute-done | bytes 147488 | tf_op jit(solution)/shard_map/ppermute | solution.py:26
  75.8 6.1 %collective-permute-done.21 = bf16[128,1024]{1,0:T(8,128)(2,1)S(1)} collective-permute-done((bf16[128,1024]{1,0:T(8,128)(2,1)S(1)}, bf16[128,1024]{1,0:T(8,128)(2,1)S(1)}, u32[]{:S(2)}, u32[]{:S(2)}) %collective-permute-start.21) | collective-permute-done | bytes 262176 | tf_op jit(solution)/shard_map/ppermute | solution.py:26
  82.2 1.7 %fusion.36 = f32[128,2304]{1,0:T(8,128)S(1)} fusion(bf16[128,1024]{1,0:T(8,128)(2,1)S(1)} %get-tuple-element.56.codes_b, bf16[2304,1024]{1,0:T(8,128)(2,1)S(1)} %bitcast.22), kind=kOutput, calls=%fused_computation.130 | convolution fusion | flops 603979776 | bytes 6160384 | tf_op jit(solution)/shard_map/dot_general | solution.py:361
  84.0 3.1 %collective-permute-done.22 = bf16[128,1024]{1,0:T(8,128)(2,1)S(1)} collective-permute-done((bf16[128,1024]{1,0:T(8,128)(2,1)S(1)}, bf16[128,1024]{1,0:T(8,128)(2,1)S(1)}, u32[]{:S(2)}, u32[]{:S(2)}) %collective-permute-start.22) | collective-permute-done | bytes 262176 | tf_op jit(solution)/shard_map/ppermute | solution.py:26
  87.3 1.7 %fusion.35 = f32[128,2304]{1,0:T(8,128)S(1)} fusion(bf16[128,1024]{1,0:T(8,128)(2,1)S(1)} %get-tuple-element.59.codes_a, bf16[2304,1024]{1,0:T(8,128)(2,1)S(1)} %bitcast.22), kind=kOutput, calls=%fused_computation.129 | convolution fusion | flops 603979776 | bytes 6160384 | tf_op jit(solution)/shard_map/dot_general | solution.py:361
  92.4 4.5 %collective-permute-done.29 = bf16[32,2304]{1,0:T(8,128)(2,1)S(1)} collective-permute-done((bf16[32,2304]{1,0:T(8,128)(2,1)S(1)}, bf16[32,2304]{1,0:T(8,128)(2,1)S(1)}, u32[]{:S(2)}, u32[]{:S(2)}) %collective-permute-start.29) | collective-permute-done | bytes 147488 | tf_op jit(solution)/shard_map/ppermute | solution.py:26
  98.2 2.0 %collective-permute-start.32 = (bf16[8,2304]{1,0:T(8,128)(2,1)S(1)}, bf16[8,2304]{1,0:T(8,128)(2,1)S(1)}, u32[]{:S(2)}, u32[]{:S(2)}) collective-permute-start(bf16[8,2304]{1,0:T(8,128)(2,1)S(1)} %get-tuple-element.93), channel_id=1, source_target_pairs={{0,3},{1,2},{2,1},{3,0},{4,7},{5,6},{6,5},{7,4},{8,11},{9,10},{10,... | collective-permute-start | bytes 110600 | tf_op jit(solution)/shard_map/ppermute | solution.py:26
  100.6 2.1 %collective-permute-start.25 = (bf16[8,2304]{1,0:T(8,128)(2,1)S(1)}, bf16[8,2304]{1,0:T(8,128)(2,1)S(1)}, u32[]{:S(2)}, u32[]{:S(2)}) collective-permute-start(bf16[8,2304]{1,0:T(8,128)(2,1)S(1)} %get-tuple-element.95), channel_id=1, source_target_pairs={{0,1},{1,0},{2,3},{3,2},{4,5},{5,4},{6,7},{7,6},{8,9},{9,8},{10,11... | collective-permute-start | bytes 110600 | tf_op jit(solution)/shard_map/ppermute | solution.py:26
  102.7 2.0 %collective-permute-start.27 = (bf16[8,2304]{1,0:T(8,128)(2,1)S(1)}, bf16[8,2304]{1,0:T(8,128)(2,1)S(1)}, u32[]{:S(2)}, u32[]{:S(2)}) collective-permute-start(bf16[8,2304]{1,0:T(8,128)(2,1)S(1)} %get-tuple-element.96), channel_id=1, source_target_pairs={{0,3},{1,2},{2,1},{3,0},{4,7},{5,6},{6,5},{7,4},{8,11},{9,10},{10,... | collective-permute-start | bytes 110600 | tf_op jit(solution)/shard_map/ppermute | solution.py:26
  105.1 1.9 %collective-permute-start.40 = (bf16[8,2304]{1,0:T(8,128)(2,1)S(1)}, bf16[8,2304]{1,0:T(8,128)(2,1)S(1)}, u32[]{:S(2)}, u32[]{:S(2)}) collective-permute-start(bf16[8,2304]{1,0:T(8,128)(2,1)S(1)} %fusion.13), channel_id=1, source_target_pairs={{0,3},{1,2},{2,1},{3,0},{4,7},{5,6},{6,5},{7,4},{8,11},{9,10},{10,... | collective-permute-start | bytes 110600 | tf_op jit(solution)/shard_map/ppermute | solution.py:26
  110.1 2.0 %collective-permute-start.35 = (bf16[8,2304]{1,0:T(8,128)(2,1)S(1)}, bf16[8,2304]{1,0:T(8,128)(2,1)S(1)}, u32[]{:S(2)}, u32[]{:S(2)}) collective-permute-start(bf16[8,2304]{1,0:T(8,128)(2,1)S(1)} %subtract_convert_fusion), channel_id=1, source_target_pairs={{0,3},{1,2},{2,1},{3,0},{4,7},{5,6},{6,5},{7,4},{8,11},{9,10},{10,... | collective-permute-start | bytes 110600 | tf_op jit(solution)/shard_map/ppermute | solution.py:26
  112.3 2.3 %collective-permute-start.33 = (bf16[8,2304]{1,0:T(8,128)(2,1)S(1)}, bf16[8,2304]{1,0:T(8,128)(2,1)S(1)}, u32[]{:S(2)}, u32[]{:S(2)}) collective-permute-start(bf16[8,2304]{1,0:T(8,128)(2,1)S(1)} %subtract_convert_fusion), channel_id=1, source_target_pairs={{0,1},{1,0},{2,3},{3,2},{4,5},{5,4},{6,7},{7,6},{8,9},{9,8},{10,11... | collective-permute-start | bytes 110600 | tf_op jit(solution)/shard_map/ppermute | solution.py:26
  114.6 1.7 %collective-permute-start.41 = (bf16[32,2304]{1,0:T(8,128)(2,1)S(1)}, bf16[32,2304]{1,0:T(8,128)(2,1)S(1)}, u32[]{:S(2)}, u32[]{:S(2)}) collective-permute-start(bf16[32,2304]{1,0:T(8,128)(2,1)S(1)} %pad_maximum_fusion.8._), channel_id=1, source_target_pairs={{0,8},{4,12},{8,0},{12,4},{1,9},{5,13},{9,1},{13,5},{2,10},{6,14},... | collective-permute-start | bytes 442376 | tf_op jit(solution)/shard_map/ppermute | solution.py:26
  120.0 2.3 %collective-permute-done.36 = bf16[32,2304]{1,0:T(8,128)(2,1)S(1)} collective-permute-done((bf16[32,2304]{1,0:T(8,128)(2,1)S(1)}, bf16[32,2304]{1,0:T(8,128)(2,1)S(1)}, u32[]{:S(2)}, u32[]{:S(2)}) %collective-permute-start.36) | collective-permute-done | bytes 147488 | tf_op jit(solution)/shard_map/ppermute | solution.py:26
  127.7 4.7 %collective-permute-done.43 = bf16[128,1024]{1,0:T(8,128)(2,1)S(1)} collective-permute-done((bf16[128,1024]{1,0:T(8,128)(2,1)S(1)}, bf16[128,1024]{1,0:T(8,128)(2,1)S(1)}, u32[]{:S(2)}, u32[]{:S(2)}) %collective-permute-start.43) | collective-permute-done | bytes 262176 | tf_op jit(solution)/shard_map/ppermute | solution.py:26
  132.6 5.0 %collective-permute-done.44 = bf16[128,1024]{1,0:T(8,128)(2,1)S(1)} collective-permute-done((bf16[128,1024]{1,0:T(8,128)(2,1)S(1)}, bf16[128,1024]{1,0:T(8,128)(2,1)S(1)}, u32[]{:S(2)}, u32[]{:S(2)}) %collective-permute-start.44) | collective-permute-done | bytes 262176 | tf_op jit(solution)/shard_map/ppermute | solution.py:26
  138.3 2.6 %shard_map.152 = bf16[2304,1024]{1,0:T(8,128)(2,1)} custom-call(f32[2304,1024]{1,0:T(8,128)S(1)} %get-tuple-element.63.total, bf16[2304,256]{1,0:T(8,128)(2,1)S(1)} %get-tuple-element.64.turned, bf16[128,1024]{1,0:T(8,128)(2,1)S(1)} %get-tuple-element.76.grad_a, bf16[128,1024]{1,0:T(8,128)(2,1)S(1)} %get-tuple-element.74.grad_b), custom_call_target="tpu_custom_call" | custom-call | flops 1207959552 | bytes 14155776 | tf_op jit(solution)/shard_map/pallas_call | solution.py:451
  (159 shorter events, 43.9 us)
Async XLA Ops:
  0.6 8.1 %collective-permute-start.2 = (bf16[1,288,128]{2,1,0:T(8,128)(2,1)}, bf16[1,288,128]{2,1,0:T(8,128)(2,1)S(1)}, u32[]{:S(2)}, u32[]{:S(2)}) collective-permute-start(bf16[1,288,128]{2,1,0:T(8,128)(2,1)} %bitcast.24), channel_id=1, source_target_pairs={{0,3},{1,2},{2,1},{3,0},{4,7},{5,6},{6,5},{7,4},{8,11},{9,10},{10,... | collective-permute-start | bytes 221192 | tf_op jit(solution)/shard_map/ppermute | solution.py:26
  5.8 6.4 %collective-permute-start.1 = (bf16[1,288,128]{2,1,0:T(8,128)(2,1)}, bf16[1,288,128]{2,1,0:T(8,128)(2,1)S(1)}, u32[]{:S(2)}, u32[]{:S(2)}) collective-permute-start(bf16[1,288,128]{2,1,0:T(8,128)(2,1)} %bitcast.25), channel_id=1, source_target_pairs={{0,2},{1,3},{2,0},{3,1},{4,6},{5,7},{6,4},{7,5},{8,10},{9,11},{10,... | collective-permute-start | bytes 221192 | tf_op jit(solution)/shard_map/ppermute | solution.py:26
  5.8 6.4 %collective-permute-start = (bf16[1,288,128]{2,1,0:T(8,128)(2,1)}, bf16[1,288,128]{2,1,0:T(8,128)(2,1)S(1)}, u32[]{:S(2)}, u32[]{:S(2)}) collective-permute-start(bf16[1,288,128]{2,1,0:T(8,128)(2,1)} %bitcast.26), channel_id=1, source_target_pairs={{0,1},{1,0},{2,3},{3,2},{4,5},{5,4},{6,7},{7,6},{8,9},{9,8},{10,11... | collective-permute-start | bytes 221192 | tf_op jit(solution)/shard_map/ppermute | solution.py:26
  13.1 8.4 %collective-permute-start.3 = (bf16[4,288,128]{2,1,0:T(8,128)(2,1)S(1)}, bf16[4,288,128]{2,1,0:T(8,128)(2,1)S(1)}, u32[]{:S(2)}, u32[]{:S(2)}) collective-permute-start(bf16[4,288,128]{2,1,0:T(8,128)(2,1)S(1)} %pad_maximum_fusion.2), channel_id=1, source_target_pairs={{0,8},{4,12},{8,0},{12,4},{1,9},{5,13},{9,1},{13,5},{2,10},{6,14},... | collective-permute-start | bytes 884744 | tf_op jit(solution)/shard_map/ppermute | solution.py:26
  31.5 9.1 %collective-permute-start.6 = (bf16[32,4608]{1,0:T(8,128)(2,1)S(1)}, bf16[32,4608]{1,0:T(8,128)(2,1)S(1)}, u32[]{:S(2)}, u32[]{:S(2)}) collective-permute-start(bf16[32,4608]{1,0:T(8,128)(2,1)S(1)} %slice.188), channel_id=1, source_target_pairs={{0,8},{4,12},{8,0},{12,4},{1,9},{5,13},{9,1},{13,5},{2,10},{6,14},... | collective-permute-start | bytes 884744 | tf_op jit(solution)/shard_map/ppermute | solution.py:26
  40.7 5.4 %collective-permute-start.7 = (bf16[8,4608]{1,0:T(8,128)(2,1)S(1)}, bf16[8,4608]{1,0:T(8,128)(2,1)S(1)}, u32[]{:S(2)}, u32[]{:S(2)}) collective-permute-start(bf16[8,4608]{1,0:T(8,128)(2,1)S(1)} %get-tuple-element.87), channel_id=1, source_target_pairs={{0,1},{1,0},{2,3},{3,2},{4,5},{5,4},{6,7},{7,6},{8,9},{9,8},{10,11... | collective-permute-start | bytes 221192 | tf_op jit(solution)/shard_map/ppermute | solution.py:26
  41.1 6.3 %collective-permute-start.9 = (bf16[8,4608]{1,0:T(8,128)(2,1)S(1)}, bf16[8,4608]{1,0:T(8,128)(2,1)S(1)}, u32[]{:S(2)}, u32[]{:S(2)}) collective-permute-start(bf16[8,4608]{1,0:T(8,128)(2,1)S(1)} %get-tuple-element.88), channel_id=1, source_target_pairs={{0,3},{1,2},{2,1},{3,0},{4,7},{5,6},{6,5},{7,4},{8,11},{9,10},{10,... | collective-permute-start | bytes 221192 | tf_op jit(solution)/shard_map/ppermute | solution.py:26
  42.7 7.7 %collective-permute-start.8 = (bf16[8,4608]{1,0:T(8,128)(2,1)S(1)}, bf16[8,4608]{1,0:T(8,128)(2,1)S(1)}, u32[]{:S(2)}, u32[]{:S(2)}) collective-permute-start(bf16[8,4608]{1,0:T(8,128)(2,1)S(1)} %get-tuple-element.89), channel_id=1, source_target_pairs={{0,2},{1,3},{2,0},{3,1},{4,6},{5,7},{6,4},{7,5},{8,10},{9,11},{10,... | collective-permute-start | bytes 221192 | tf_op jit(solution)/shard_map/ppermute | solution.py:26
  50.7 6.1 %collective-permute-start.12 = (bf16[8,2304]{1,0:T(8,128)(2,1)S(1)}, bf16[8,2304]{1,0:T(8,128)(2,1)S(1)}, u32[]{:S(2)}, u32[]{:S(2)}) collective-permute-start(bf16[8,2304]{1,0:T(8,128)(2,1)S(1)} %get-tuple-element.101), channel_id=1, source_target_pairs={{0,3},{1,2},{2,1},{3,0},{4,7},{5,6},{6,5},{7,4},{8,11},{9,10},{10,... | collective-permute-start | bytes 110600 | tf_op jit(solution)/shard_map/ppermute | solution.py:26
  57.5 10.5 %collective-permute-start.13 = (bf16[32,2304]{1,0:T(8,128)(2,1)S(1)}, bf16[32,2304]{1,0:T(8,128)(2,1)S(1)}, u32[]{:S(2)}, u32[]{:S(2)}) collective-permute-start(bf16[32,2304]{1,0:T(8,128)(2,1)S(1)} %pad_maximum_fusion.5._), channel_id=1, source_target_pairs={{0,8},{4,12},{8,0},{12,4},{1,9},{5,13},{9,1},{13,5},{2,10},{6,14},... | collective-permute-start | bytes 442376 | tf_op jit(solution)/shard_map/ppermute | solution.py:26
  59.2 7.1 %collective-permute-start.18 = (bf16[8,2304]{1,0:T(8,128)(2,1)S(1)}, bf16[8,2304]{1,0:T(8,128)(2,1)S(1)}, u32[]{:S(2)}, u32[]{:S(2)}) collective-permute-start(bf16[8,2304]{1,0:T(8,128)(2,1)S(1)} %collective-permute-done.15), channel_id=1, source_target_pairs={{0,3},{1,2},{2,1},{3,0},{4,7},{5,6},{6,5},{7,4},{8,11},{9,10},{10,... | collective-permute-start | bytes 110600 | tf_op jit(solution)/shard_map/ppermute | solution.py:26
  61.2 5.3 %collective-permute-start.17 = (bf16[8,2304]{1,0:T(8,128)(2,1)S(1)}, bf16[8,2304]{1,0:T(8,128)(2,1)S(1)}, u32[]{:S(2)}, u32[]{:S(2)}) collective-permute-start(bf16[8,2304]{1,0:T(8,128)(2,1)S(1)} %collective-permute-done.15), channel_id=1, source_target_pairs={{0,2},{1,3},{2,0},{3,1},{4,6},{5,7},{6,4},{7,5},{8,10},{9,11},{10,... | collective-permute-start | bytes 110600 | tf_op jit(solution)/shard_map/ppermute | solution.py:26
  66.5 5.2 %collective-permute-start.19 = (bf16[32,2304]{1,0:T(8,128)(2,1)S(1)}, bf16[32,2304]{1,0:T(8,128)(2,1)S(1)}, u32[]{:S(2)}, u32[]{:S(2)}) collective-permute-start(bf16[32,2304]{1,0:T(8,128)(2,1)S(1)} %pad_maximum_fusion.6), channel_id=1, source_target_pairs={{0,8},{4,12},{8,0},{12,4},{1,9},{5,13},{9,1},{13,5},{2,10},{6,14},... | collective-permute-start | bytes 442376 | tf_op jit(solution)/shard_map/ppermute | solution.py:26
  72.7 9.2 %collective-permute-start.21 = (bf16[128,1024]{1,0:T(8,128)(2,1)S(1)}, bf16[128,1024]{1,0:T(8,128)(2,1)S(1)}, u32[]{:S(2)}, u32[]{:S(2)}) collective-permute-start(bf16[128,1024]{1,0:T(8,128)(2,1)S(1)} %get-tuple-element.55), channel_id=1, source_target_pairs={{0,16},{16,0},{1,17},{17,1},{2,18},{18,2},{3,19},{19,3},{4,20},{20... | collective-permute-start | bytes 786440 | tf_op jit(solution)/shard_map/ppermute | solution.py:26
  75.1 11.9 %collective-permute-start.22 = (bf16[128,1024]{1,0:T(8,128)(2,1)S(1)}, bf16[128,1024]{1,0:T(8,128)(2,1)S(1)}, u32[]{:S(2)}, u32[]{:S(2)}) collective-permute-start(bf16[128,1024]{1,0:T(8,128)(2,1)S(1)} %get-tuple-element.57), channel_id=1, source_target_pairs={{0,16},{16,0},{1,17},{17,1},{2,18},{18,2},{3,19},{19,3},{4,20},{20... | collective-permute-start | bytes 786440 | tf_op jit(solution)/shard_map/ppermute | solution.py:26
  83.9 6.2 %collective-permute-start.28 = (bf16[64,2304]{1,0:T(8,128)(2,1)S(1)}, bf16[64,2304]{1,0:T(8,128)(2,1)S(1)}, u32[]{:S(2)}, u32[]{:S(2)}) collective-permute-start(bf16[64,2304]{1,0:T(8,128)(2,1)S(1)} %slice.186), channel_id=1, source_target_pairs={{0,4},{4,0},{8,12},{12,8},{1,5},{5,1},{9,13},{13,9},{2,6},{6,2},{1... | collective-permute-start | bytes 884744 | tf_op jit(solution)/shard_map/ppermute | solution.py:26
  90.2 6.8 %collective-permute-start.29 = (bf16[32,2304]{1,0:T(8,128)(2,1)S(1)}, bf16[32,2304]{1,0:T(8,128)(2,1)S(1)}, u32[]{:S(2)}, u32[]{:S(2)}) collective-permute-start(bf16[32,2304]{1,0:T(8,128)(2,1)S(1)} %slice.189), channel_id=1, source_target_pairs={{0,8},{4,12},{8,0},{12,4},{1,9},{5,13},{9,1},{13,5},{2,10},{6,14},... | collective-permute-start | bytes 442376 | tf_op jit(solution)/shard_map/ppermute | solution.py:26
  91.8 8.8 %collective-permute-start.24 = (bf16[32,2304]{1,0:T(8,128)(2,1)S(1)}, bf16[32,2304]{1,0:T(8,128)(2,1)S(1)}, u32[]{:S(2)}, u32[]{:S(2)}) collective-permute-start(bf16[32,2304]{1,0:T(8,128)(2,1)S(1)} %slice.190), channel_id=1, source_target_pairs={{0,8},{4,12},{8,0},{12,4},{1,9},{5,13},{9,1},{13,5},{2,10},{6,14},... | collective-permute-start | bytes 442376 | tf_op jit(solution)/shard_map/ppermute | solution.py:26
  97.0 7.6 %collective-permute-start.30 = (bf16[8,2304]{1,0:T(8,128)(2,1)S(1)}, bf16[8,2304]{1,0:T(8,128)(2,1)S(1)}, u32[]{:S(2)}, u32[]{:S(2)}) collective-permute-start(bf16[8,2304]{1,0:T(8,128)(2,1)S(1)} %get-tuple-element.92), channel_id=1, source_target_pairs={{0,1},{1,0},{2,3},{3,2},{4,5},{5,4},{6,7},{7,6},{8,9},{9,8},{10,11... | collective-permute-start | bytes 110600 | tf_op jit(solution)/shard_map/ppermute | solution.py:26
  98.2 6.5 %collective-permute-start.32 = (bf16[8,2304]{1,0:T(8,128)(2,1)S(1)}, bf16[8,2304]{1,0:T(8,128)(2,1)S(1)}, u32[]{:S(2)}, u32[]{:S(2)}) collective-permute-start(bf16[8,2304]{1,0:T(8,128)(2,1)S(1)} %get-tuple-element.93), channel_id=1, source_target_pairs={{0,3},{1,2},{2,1},{3,0},{4,7},{5,6},{6,5},{7,4},{8,11},{9,10},{10,... | collective-permute-start | bytes 110600 | tf_op jit(solution)/shard_map/ppermute | solution.py:26
  100.1 5.0 %collective-permute-start.31 = (bf16[8,2304]{1,0:T(8,128)(2,1)S(1)}, bf16[8,2304]{1,0:T(8,128)(2,1)S(1)}, u32[]{:S(2)}, u32[]{:S(2)}) collective-permute-start(bf16[8,2304]{1,0:T(8,128)(2,1)S(1)} %get-tuple-element.94), channel_id=1, source_target_pairs={{0,2},{1,3},{2,0},{3,1},{4,6},{5,7},{6,4},{7,5},{8,10},{9,11},{10,... | collective-permute-start | bytes 110600 | tf_op jit(solution)/shard_map/ppermute | solution.py:26
  100.6 8.0 %collective-permute-start.25 = (bf16[8,2304]{1,0:T(8,128)(2,1)S(1)}, bf16[8,2304]{1,0:T(8,128)(2,1)S(1)}, u32[]{:S(2)}, u32[]{:S(2)}) collective-permute-start(bf16[8,2304]{1,0:T(8,128)(2,1)S(1)} %get-tuple-element.95), channel_id=1, source_target_pairs={{0,1},{1,0},{2,3},{3,2},{4,5},{5,4},{6,7},{7,6},{8,9},{9,8},{10,11... | collective-permute-start | bytes 110600 | tf_op jit(solution)/shard_map/ppermute | solution.py:26
  102.7 6.9 %collective-permute-start.27 = (bf16[8,2304]{1,0:T(8,128)(2,1)S(1)}, bf16[8,2304]{1,0:T(8,128)(2,1)S(1)}, u32[]{:S(2)}, u32[]{:S(2)}) collective-permute-start(bf16[8,2304]{1,0:T(8,128)(2,1)S(1)} %get-tuple-element.96), channel_id=1, source_target_pairs={{0,3},{1,2},{2,1},{3,0},{4,7},{5,6},{6,5},{7,4},{8,11},{9,10},{10,... | collective-permute-start | bytes 110600 | tf_op jit(solution)/shard_map/ppermute | solution.py:26
  104.6 5.4 %collective-permute-start.26 = (bf16[8,2304]{1,0:T(8,128)(2,1)S(1)}, bf16[8,2304]{1,0:T(8,128)(2,1)S(1)}, u32[]{:S(2)}, u32[]{:S(2)}) collective-permute-start(bf16[8,2304]{1,0:T(8,128)(2,1)S(1)} %get-tuple-element.97), channel_id=1, source_target_pairs={{0,2},{1,3},{2,0},{3,1},{4,6},{5,7},{6,4},{7,5},{8,10},{9,11},{10,... | collective-permute-start | bytes 110600 | tf_op jit(solution)/shard_map/ppermute | solution.py:26
  105.1 7.1 %collective-permute-start.40 = (bf16[8,2304]{1,0:T(8,128)(2,1)S(1)}, bf16[8,2304]{1,0:T(8,128)(2,1)S(1)}, u32[]{:S(2)}, u32[]{:S(2)}) collective-permute-start(bf16[8,2304]{1,0:T(8,128)(2,1)S(1)} %fusion.13), channel_id=1, source_target_pairs={{0,3},{1,2},{2,1},{3,0},{4,7},{5,6},{6,5},{7,4},{8,11},{9,10},{10,... | collective-permute-start | bytes 110600 | tf_op jit(solution)/shard_map/ppermute | solution.py:26
  107.1 7.5 %collective-permute-start.39 = (bf16[8,2304]{1,0:T(8,128)(2,1)S(1)}, bf16[8,2304]{1,0:T(8,128)(2,1)S(1)}, u32[]{:S(2)}, u32[]{:S(2)}) collective-permute-start(bf16[8,2304]{1,0:T(8,128)(2,1)S(1)} %fusion.13), channel_id=1, source_target_pairs={{0,2},{1,3},{2,0},{3,1},{4,6},{5,7},{6,4},{7,5},{8,10},{9,11},{10,... | collective-permute-start | bytes 110600 | tf_op jit(solution)/shard_map/ppermute | solution.py:26
  108.6 6.0 %collective-permute-start.38 = (bf16[8,2304]{1,0:T(8,128)(2,1)S(1)}, bf16[8,2304]{1,0:T(8,128)(2,1)S(1)}, u32[]{:S(2)}, u32[]{:S(2)}) collective-permute-start(bf16[8,2304]{1,0:T(8,128)(2,1)S(1)} %fusion.13), channel_id=1, source_target_pairs={{0,1},{1,0},{2,3},{3,2},{4,5},{5,4},{6,7},{7,6},{8,9},{9,8},{10,11... | collective-permute-start | bytes 110600 | tf_op jit(solution)/shard_map/ppermute | solution.py:26
  110.1 6.7 %collective-permute-start.35 = (bf16[8,2304]{1,0:T(8,128)(2,1)S(1)}, bf16[8,2304]{1,0:T(8,128)(2,1)S(1)}, u32[]{:S(2)}, u32[]{:S(2)}) collective-permute-start(bf16[8,2304]{1,0:T(8,128)(2,1)S(1)} %subtract_convert_fusion), channel_id=1, source_target_pairs={{0,3},{1,2},{2,1},{3,0},{4,7},{5,6},{6,5},{7,4},{8,11},{9,10},{10,... | collective-permute-start | bytes 110600 | tf_op jit(solution)/shard_map/ppermute | solution.py:26
  114.6 5.2 %collective-permute-start.41 = (bf16[32,2304]{1,0:T(8,128)(2,1)S(1)}, bf16[32,2304]{1,0:T(8,128)(2,1)S(1)}, u32[]{:S(2)}, u32[]{:S(2)}) collective-permute-start(bf16[32,2304]{1,0:T(8,128)(2,1)S(1)} %pad_maximum_fusion.8._), channel_id=1, source_target_pairs={{0,8},{4,12},{8,0},{12,4},{1,9},{5,13},{9,1},{13,5},{2,10},{6,14},... | collective-permute-start | bytes 442376 | tf_op jit(solution)/shard_map/ppermute | solution.py:26
  117.0 5.2 %collective-permute-start.36 = (bf16[32,2304]{1,0:T(8,128)(2,1)S(1)}, bf16[32,2304]{1,0:T(8,128)(2,1)S(1)}, u32[]{:S(2)}, u32[]{:S(2)}) collective-permute-start(bf16[32,2304]{1,0:T(8,128)(2,1)S(1)} %pad_maximum_fusion.7), channel_id=1, source_target_pairs={{0,8},{4,12},{8,0},{12,4},{1,9},{5,13},{9,1},{13,5},{2,10},{6,14},... | collective-permute-start | bytes 442376 | tf_op jit(solution)/shard_map/ppermute | solution.py:26
  123.2 9.2 %collective-permute-start.43 = (bf16[128,1024]{1,0:T(8,128)(2,1)S(1)}, bf16[128,1024]{1,0:T(8,128)(2,1)S(1)}, u32[]{:S(2)}, u32[]{:S(2)}) collective-permute-start(bf16[128,1024]{1,0:T(8,128)(2,1)S(1)} %get-tuple-element.67), channel_id=1, source_target_pairs={{0,16},{16,0},{1,17},{17,1},{2,18},{18,2},{3,19},{19,3},{4,20},{20... | collective-permute-start | bytes 786440 | tf_op jit(solution)/shard_map/ppermute | solution.py:26
  125.6 12.0 %collective-permute-start.44 = (bf16[128,1024]{1,0:T(8,128)(2,1)S(1)}, bf16[128,1024]{1,0:T(8,128)(2,1)S(1)}, u32[]{:S(2)}, u32[]{:S(2)}) collective-permute-start(bf16[128,1024]{1,0:T(8,128)(2,1)S(1)} %get-tuple-element.70), channel_id=1, source_target_pairs={{0,16},{16,0},{1,17},{17,1},{2,18},{18,2},{3,19},{19,3},{4,20},{20... | collective-permute-start | bytes 786440 | tf_op jit(solution)/shard_map/ppermute | solution.py:26
  (25 other events, 188.1 us)
where the time goes:
time: 141 us
  waiting for transfers between devices  60.1 us (43%)
  starting transfers between devices  53.4 us (38%)
  Pallas kernels  8.69 us (6%)
  matrix products  7.5 us (5%)
  other arithmetic  5.44 us (4%)
  local copies, waits for them, and re-layouts  4.42 us (3%)
  between operations  1.41 us (1%)
    ppermute x45, waiting for transfers between devices, swap(): return lax.ppermute(values, axis, [(i, i ^ mask) for i in range(size)])  60.1 us
    ppermute x45, starting transfers between devices, swap(): return lax.ppermute(values, axis, [(i, i ^ mask) for i in range(size)])  53.4 us
    pallas_call x1, Pallas kernels, attention(): pl.pallas_call(lambda *refs: attention_body(sizes, *refs), out_shape=(jax...  3.88 us
    dot_general x2, matrix products, rebuild(): lax.dot_general(codes[chunk], sae_weight, contract_last, preferred_elemen...  3.34 us
    dot_general x4, matrix products, partial_pair(): jnp.dot(values, weights.get(label, sae_weight), preferred_element_type=F32)  3.18 us
  transfers between devices with their start and end apart: 45, of which 22 were waited for; matrix products, arithmetic and copies ran while one was open for 8% of the time, Pallas kernels for 2%

commit v1 on v0

--- a/solution.py
+++ b/solution.py
@@ -59,9 +59,10 @@
 
 def add_arrived(kept, sent, stage):
     axis, masks = stage
+    arrived = [swap(part, axis, m) for m, part in zip(masks, sent)]
     total = kept
-    for m, part in zip(masks, sent):
-        total = total + swap(part, axis, m).astype(F32)
+    for part in arrived:
+        total = total + part.astype(F32)
     return total
 
 
@@ -279,6 +280,11 @@
     t_of, z_of = flat // latent, flat % latent
     number = ((t_of % cores) * (tensor // cores) + t_of // cores) * latent + z_of
     tables += [number ^ me, flat ^ me]
+    place = row_perm ^ ((mine * plane + me) * rows)
+    chosen = (place[:, None] == jnp.arange(length * groups, dtype=jnp.int32)[None, :]).astype(BF)
+    starts = [(mine ^ k) * half for k in range(groups)]
+    half_bias = lax.dynamic_slice(dec_bias, (starts[0],), (half,), allow_negative_indices=False)
+    tables += [chosen, half_bias] + starts
 
     def gate(pieces):
         held = lax.optimization_barrier(pieces + tables)
@@ -287,16 +293,18 @@
 
     blocks = gather_blocks(residual.T[None], gate)
     kept_rows, sent_rows, own = attention(
-        blocks, tables[-2], tables[-1], tables[:-2], (w_query, w_key, w_value, w_out)
+        blocks, tables[5], tables[6], tables[:5], (w_query, w_key, w_value, w_out)
     )
+    chosen, half_bias, *starts = tables[7:]
     attn_out = add_arrived(kept_rows, [sent_rows], plane_stages()[0])
     attn_out = scatter_sum(attn_out, 1)
     scale = lax.rsqrt(jnp.mean(attn_out * attn_out, axis=-1, keepdims=True) + epsilon)
     hidden = (own + attn_out * scale * post_gain).astype(BF)
-    pieces = hidden.reshape(rows, groups, half).transpose(1, 0, 2)
 
     def piece(k):
-        return lax.dynamic_index_in_dim(pieces, mine ^ k, 0, keepdims=False)
+        return lax.dynamic_slice(
+            hidden, (0, starts[k]), (rows, half), allow_negative_indices=False
+        )
 
     others = jnp.stack([swap(piece(k), "dp", k) for k in range(1, groups)], 0)
 
@@ -355,14 +363,17 @@
     _, first_arrived = lax.optimization_barrier((codes[1], first_arrived))
     codes[0], slopes[0] = opened(first_part, first_arrived)
 
-    half_bias = lax.dynamic_slice(dec_bias, (mine * half,), (half,))
-
     def rebuild(chunk, count, after):
-        part = lax.dot_general(codes[chunk], sae_weight, contract_last, preferred_element_type=F32)
-        if count > 1:
+        if count == 1:
+            kept, sent = rebuild_split(codes[chunk], sae_weight)
+            total = add_arrived(kept, [sent], plane_stages()[0])
+            total = scatter_sum(total, 1)
+        else:
+            part = lax.dot_general(
+                codes[chunk], sae_weight, contract_last, preferred_element_type=F32
+            )
             part = part.reshape(count, plane, rows, half).transpose(1, 0, 2, 3)
-            part = part.reshape(plane * count * rows, half)
-        total = scatter_sum(part)
+            total = scatter_sum(part.reshape(plane * count * rows, half))
         if count > 1:
             held = sae[chunk].reshape(count, plane, rows, half)[:, 0].reshape(count * rows, half)
         else:
@@ -387,13 +398,36 @@
     _, rest_arrived = lax.optimization_barrier((grad_pre[0], rest_arrived))
     grad_pre[1] = ((rest + rest_arrived.astype(F32)) * slopes[1]).astype(BF)
     total, hidden_t = early_gradient(error, codes, sae)
-    weight_grad = late_gradient(total, hidden_t, grad_pre, grad_scale)
-    bias_grad = grad_scale * sum(jnp.sum(g.astype(F32), axis=0) for g in grad_pre)
-
-    place = row_perm ^ ((mine * plane + me) * rows)
-    chosen = (place[:, None] == jnp.arange(length * groups, dtype=jnp.int32)[None, :]).astype(BF)
+    weight_grad, bias_grad = late_gradient(total, hidden_t, grad_pre, grad_scale)
     out_codes = jnp.dot(chosen, jnp.concatenate(codes, 0), preferred_element_type=F32).astype(BF)
-    return (weight_grad, bias_grad, out_codes)
+    return (weight_grad, bias_grad.reshape(-1), out_codes)
+
+
+def rebuild_split(codes, weight):
+    count, half = codes.shape[0], weight.shape[0]
+    middle = count // 2
+
+    def body(codes, weight, kept, sent):
+        product = lax.dot_general(
+            codes[...], weight[...], (((1,), (1,)), ((), ())), preferred_element_type=F32
+        )
+        kept[...] = product[:middle]
+        sent[...] = product[middle:].astype(BF)
+
+    vmem = pl.BlockSpec(memory_space=pltpu.VMEM)
+    return pl.pallas_call(
+        body,
+        out_shape=(
+            jax.ShapeDtypeStruct((middle, half), F32),
+            jax.ShapeDtypeStruct((count - middle, half), BF),
+        ),
+        in_specs=[vmem] * 2,
+        out_specs=(vmem,) * 2,
+        compiler_params=pltpu.CompilerParams(vmem_limit_bytes=16 * 1024 * 1024),
+        cost_estimate=pl.CostEstimate(
+            flops=2 * count * weight.size, bytes_accessed=2 * weight.size, transcendentals=0
+        ),
+    )(codes, weight)
 
 
 def early_gradient(error, codes, hidden):
@@ -431,7 +465,7 @@
 
     steps = half // tile
 
-    def body(total, turned, grad_a, grad_b, out, right, ready, sems):
+    def body(total, turned, grad_a, grad_b, out, bias, right, ready, sems):
         right[:first] = grad_a[...]
         right[first:] = grad_b[...]
 
@@ -444,15 +478,22 @@
             product = jnp.dot(turned[part], right[...], preferred_element_type=F32)
             ready[part] = (grad_scale * (total[part] + product)).astype(BF)
             put(i).start()
+        bias[...] = grad_scale * (
+            jnp.sum(grad_a[...].astype(F32), axis=0, keepdims=True)
+            + jnp.sum(grad_b[...].astype(F32), axis=0, keepdims=True)
+        )
         for i in range(steps):
             put(i).wait()
 
     vmem = pl.BlockSpec(memory_space=pltpu.VMEM)
     return pl.pallas_call(
         body,
-        out_shape=jax.ShapeDtypeStruct((half, latents), BF),
+        out_shape=(
+            jax.ShapeDtypeStruct((half, latents), BF),
+            jax.ShapeDtypeStruct((1, latents), F32),
+        ),
         in_specs=[vmem] * 4,
-        out_specs=pl.BlockSpec(memory_space=pltpu.HBM),
+        out_specs=(pl.BlockSpec(memory_space=pltpu.HBM), vmem),
         scratch_shapes=[
             pltpu.VMEM((turned.shape[1], latents), BF),
             pltpu.VMEM((half, latents), BF),

time: 141 us -> 141 us (level)
  Pallas kernels: 8.69 us -> 12.6 us
  matrix products: 7.5 us -> 4.2 us
  local copies, waits for them, and re-layouts: 4.42 us -> 2.81 us
  waiting for transfers between devices: 60.1 us -> 61.7 us
    pallas_call x1 -> x3, Pallas kernels: 2.55 us -> 6.41 us  [the longest x2 3.26 us: rebuild_split(): pl.pallas_call(body, out_shape=(jax.ShapeDtypeStruct((middle, half), F32)...]
    dot_general x2 -> x0, matrix products: 3.34 us -> none  [rebuild(): lax.dot_general(codes[chunk], sae_weight, contract_last, preferred_elemen...]
    unnamed x36 -> x30, local copies, waits for them, and re-layouts: 2.49 us -> 0.15 us
    ppermute x45, waiting for transfers between devices: 60.1 us -> 61.7 us  [swap(): return lax.ppermute(values, axis, [(i, i ^ mask) for i in range(size)])]
  transfers between devices with their start and end apart: 45 -> 45, of which waited for: 22 -> 22; matrix products, arithmetic and copies ran while one was open for 8% -> 7% of each run, Pallas kernels for 2% -> 4%
where the time goes in v1:
time: 141 us
  waiting for transfers between devices  61.7 us (44%)
  starting transfers between devices  52.8 us (37%)
  Pallas kernels  12.6 us (9%)
  other arithmetic  5.58 us (4%)
  matrix products  4.2 us (3%)
  local copies, waits for them, and re-layouts  2.81 us (2%)
    ppermute x45, waiting for transfers between devices, swap(): return lax.ppermute(values, axis, [(i, i ^ mask) for i in range(size)])  61.7 us
    ppermute x45, starting transfers between devices, swap(): return lax.ppermute(values, axis, [(i, i ^ mask) for i in range(size)])  52.8 us
    pallas_call x1, Pallas kernels, attention(): pl.pallas_call(lambda *refs: attention_body(sizes, *refs), out_shape=(jax...  3.88 us
    pallas_call x2, Pallas kernels, rebuild_split(): pl.pallas_call(body, out_shape=(jax.ShapeDtypeStruct((middle, half), F32)...  3.26 us
    dot_general x4, matrix products, partial_pair(): jnp.dot(values, weights.get(label, sae_weight), preferred_element_type=F32)  3.26 us
    pallas_call x1, Pallas kernels, late_gradient(): pl.pallas_call(body, out_shape=(jax.ShapeDtypeStruct((half, latents), BF)...  3.15 us
  transfers between devices with their start and end apart: 45, of which 22 were waited for; matrix products, arithmetic and copies ran while one was open for 7% of the time, Pallas kernels for 4%

profile of v1, /device:TPU:0, one launch (start us, length us, event | category | flops | bytes accessed | tf_op | source)
XLA Modules:
  0.0 141.0 jit_solution(9447486675954288778)
XLA Ops:
  0.6 5.1 %collective-permute-start.2 = (bf16[1,288,128]{2,1,0:T(8,128)(2,1)}, bf16[1,288,128]{2,1,0:T(8,128)(2,1)S(1)}, u32[]{:S(2)}, u32[]{:S(2)}) collective-permute-start(bf16[1,288,128]{2,1,0:T(8,128)(2,1)} %bitcast.16), channel_id=1, source_target_pairs={{0,3},{1,2},{2,1},{3,0},{4,7},{5,6},{6,5},{7,4},{8,11},{9,10},{10,... | collective-permute-start | bytes 221192 | tf_op jit(solution)/shard_map/ppermute | solution.py:26
  9.4 2.8 %collective-permute-done.1 = bf16[1,288,128]{2,1,0:T(8,128)(2,1)S(1)} collective-permute-done((bf16[1,288,128]{2,1,0:T(8,128)(2,1)}, bf16[1,288,128]{2,1,0:T(8,128)(2,1)S(1)}, u32[]{:S(2)}, u32[]{:S(2)}) %collective-permute-start.1) | collective-permute-done | bytes 73760 | tf_op jit(solution)/shard_map/ppermute | solution.py:26
  13.1 1.6 %collective-permute-start.3 = (bf16[4,288,128]{2,1,0:T(8,128)(2,1)S(1)}, bf16[4,288,128]{2,1,0:T(8,128)(2,1)S(1)}, u32[]{:S(2)}, u32[]{:S(2)}) collective-permute-start(bf16[4,288,128]{2,1,0:T(8,128)(2,1)S(1)} %pad_maximum_fusion.2), channel_id=1, source_target_pairs={{0,8},{4,12},{8,0},{12,4},{1,9},{5,13},{9,1},{13,5},{2,10},{6,14},... | collective-permute-start | bytes 884744 | tf_op jit(solution)/shard_map/ppermute | solution.py:26
  15.6 6.0 %collective-permute-done.3 = bf16[4,288,128]{2,1,0:T(8,128)(2,1)S(1)} collective-permute-done((bf16[4,288,128]{2,1,0:T(8,128)(2,1)S(1)}, bf16[4,288,128]{2,1,0:T(8,128)(2,1)S(1)}, u32[]{:S(2)}, u32[]{:S(2)}) %collective-permute-start.3) | collective-permute-done | bytes 294944 | tf_op jit(solution)/shard_map/ppermute | solution.py:26
  23.2 2.0 %collective-permute-done.4 = bf16[8,288,128]{2,1,0:T(8,128)(2,1)S(1)} collective-permute-done((bf16[8,288,128]{2,1,0:T(8,128)(2,1)S(1)}, bf16[8,288,128]{2,1,0:T(8,128)(2,1)S(1)}, u32[]{:S(2)}, u32[]{:S(2)}) %collective-permute-start.4) | collective-permute-done | bytes 589856 | tf_op jit(solution)/shard_map/ppermute | solution.py:26
  25.4 3.9 %shard_map.148 = (f32[64,4608]{1,0:T(8,128)S(1)}, bf16[64,4608]{1,0:T(8,128)(2,1)S(1)}, f32[8,4608]{1,0:T(8,128)S(1)}) custom-call(s32[16]{0:T(128)S(1)} %get-tuple-element.48.refs_0_, s32[16]{0:T(128)S(1)} %get-tuple-element.49.refs_1_, bf16[16,288,128]{2,1,0:T(8,128)(2,1)S(1)} %pad_maximum_fusion.refs_2_, f32[4608,128]{1,0:T(8,128)S(1)} %broadcast_in_dim.5.refs_3_, ...), custom_call_target="tpu_custom_call" | custom-call | flops 905969664 | bytes 7077888 | tf_op jit(solution)/shard_map/pallas_call | solution.py:217
  29.5 1.9 %collective-permute-done.5 = bf16[64,4608]{1,0:T(8,128)(2,1)S(1)} collective-permute-done((bf16[64,4608]{1,0:T(8,128)(2,1)S(1)}, bf16[64,4608]{1,0:T(8,128)(2,1)S(1)}, u32[]{:S(2)}, u32[]{:S(2)}) %collective-permute-start.5) | collective-permute-done | bytes 589856 | tf_op jit(solution)/shard_map/ppermute | solution.py:26
  31.6 1.8 %collective-permute-start.6 = (bf16[32,4608]{1,0:T(8,128)(2,1)S(1)}, bf16[32,4608]{1,0:T(8,128)(2,1)S(1)}, u32[]{:S(2)}, u32[]{:S(2)}) collective-permute-start(bf16[32,4608]{1,0:T(8,128)(2,1)S(1)} %slice.156), channel_id=1, source_target_pairs={{0,8},{4,12},{8,0},{12,4},{1,9},{5,13},{9,1},{13,5},{2,10},{6,14},... | collective-permute-start | bytes 884744 | tf_op jit(solution)/shard_map/ppermute | solution.py:26
  33.3 7.4 %collective-permute-done.6 = bf16[32,4608]{1,0:T(8,128)(2,1)S(1)} collective-permute-done((bf16[32,4608]{1,0:T(8,128)(2,1)S(1)}, bf16[32,4608]{1,0:T(8,128)(2,1)S(1)}, u32[]{:S(2)}, u32[]{:S(2)}) %collective-permute-start.6) | collective-permute-done | bytes 294944 | tf_op jit(solution)/shard_map/ppermute | solution.py:26
  44.3 1.9 %collective-permute-done.7 = bf16[8,4608]{1,0:T(8,128)(2,1)S(1)} collective-permute-done((bf16[8,4608]{1,0:T(8,128)(2,1)S(1)}, bf16[8,4608]{1,0:T(8,128)(2,1)S(1)}, u32[]{:S(2)}, u32[]{:S(2)}) %collective-permute-start.7) | collective-permute-done | bytes 73760 | tf_op jit(solution)/shard_map/ppermute | solution.py:26
  47.5 3.0 %collective-permute-done.8 = bf16[8,4608]{1,0:T(8,128)(2,1)S(1)} collective-permute-done((bf16[8,4608]{1,0:T(8,128)(2,1)S(1)}, bf16[8,4608]{1,0:T(8,128)(2,1)S(1)}, u32[]{:S(2)}, u32[]{:S(2)}) %collective-permute-start.8) | collective-permute-done | bytes 73760 | tf_op jit(solution)/shard_map/ppermute | solution.py:26
  50.8 1.9 %collective-permute-start.12 = (bf16[8,2304]{1,0:T(8,128)(2,1)S(1)}, bf16[8,2304]{1,0:T(8,128)(2,1)S(1)}, u32[]{:S(2)}, u32[]{:S(2)}) collective-permute-start(bf16[8,2304]{1,0:T(8,128)(2,1)S(1)} %get-tuple-element.117), channel_id=1, source_target_pairs={{0,3},{1,2},{2,1},{3,0},{4,7},{5,6},{6,5},{7,4},{8,11},{9,10},{10,... | collective-permute-start | bytes 110600 | tf_op jit(solution)/shard_map/ppermute | solution.py:26
  52.7 2.5 %collective-permute-start.10 = (bf16[8,2304]{1,0:T(8,128)(2,1)S(1)}, bf16[8,2304]{1,0:T(8,128)(2,1)S(1)}, u32[]{:S(2)}, u32[]{:S(2)}) collective-permute-start(bf16[8,2304]{1,0:T(8,128)(2,1)S(1)} %get-tuple-element.117), channel_id=1, source_target_pairs={{0,1},{1,0},{2,3},{3,2},{4,5},{5,4},{6,7},{7,6},{8,9},{9,8},{10,11... | collective-permute-start | bytes 110600 | tf_op jit(solution)/shard_map/ppermute | solution.py:26
  57.6 1.7 %collective-permute-start.13 = (bf16[32,2304]{1,0:T(8,128)(2,1)S(1)}, bf16[32,2304]{1,0:T(8,128)(2,1)S(1)}, u32[]{:S(2)}, u32[]{:S(2)}) collective-permute-start(bf16[32,2304]{1,0:T(8,128)(2,1)S(1)} %pad_maximum_fusion.5._), channel_id=1, source_target_pairs={{0,8},{4,12},{8,0},{12,4},{1,9},{5,13},{9,1},{13,5},{2,10},{6,14},... | collective-permute-start | bytes 442376 | tf_op jit(solution)/shard_map/ppermute | solution.py:26
  59.3 2.0 %collective-permute-start.18 = (bf16[8,2304]{1,0:T(8,128)(2,1)S(1)}, bf16[8,2304]{1,0:T(8,128)(2,1)S(1)}, u32[]{:S(2)}, u32[]{:S(2)}) collective-permute-start(bf16[8,2304]{1,0:T(8,128)(2,1)S(1)} %collective-permute-done.15), channel_id=1, source_target_pairs={{0,3},{1,2},{2,1},{3,0},{4,7},{5,6},{6,5},{7,4},{8,11},{9,10},{10,... | collective-permute-start | bytes 110600 | tf_op jit(solution)/shard_map/ppermute | solution.py:26
  67.9 4.0 %collective-permute-done.19 = bf16[32,2304]{1,0:T(8,128)(2,1)S(1)} collective-permute-done((bf16[32,2304]{1,0:T(8,128)(2,1)S(1)}, bf16[32,2304]{1,0:T(8,128)(2,1)S(1)}, u32[]{:S(2)}, u32[]{:S(2)}) %collective-permute-start.19) | collective-permute-done | bytes 147488 | tf_op jit(solution)/shard_map/ppermute | solution.py:26
  75.9 6.1 %collective-permute-done.21 = bf16[128,1024]{1,0:T(8,128)(2,1)S(1)} collective-permute-done((bf16[128,1024]{1,0:T(8,128)(2,1)S(1)}, bf16[128,1024]{1,0:T(8,128)(2,1)S(1)}, u32[]{:S(2)}, u32[]{:S(2)}) %collective-permute-start.21) | collective-permute-done | bytes 262176 | tf_op jit(solution)/shard_map/ppermute | solution.py:26
  82.3 1.6 %shard_map.151 = (f32[64,2304]{1,0:T(8,128)S(1)}, bf16[64,2304]{1,0:T(8,128)(2,1)S(1)}) custom-call(bf16[128,1024]{1,0:T(8,128)(2,1)S(1)} %get-tuple-element.68.codes.codes_b, bf16[2304,1024]{1,0:T(8,128)(2,1)S(1)} %bitcast.15), custom_call_target="tpu_custom_call" | custom-call | flops 603979776 | bytes 4718592 | tf_op jit(solution)/shard_map/pallas_call | solution.py:418
  84.0 3.1 %collective-permute-done.22 = bf16[128,1024]{1,0:T(8,128)(2,1)S(1)} collective-permute-done((bf16[128,1024]{1,0:T(8,128)(2,1)S(1)}, bf16[128,1024]{1,0:T(8,128)(2,1)S(1)}, u32[]{:S(2)}, u32[]{:S(2)}) %collective-permute-start.22) | collective-permute-done | bytes 262176 | tf_op jit(solution)/shard_map/ppermute | solution.py:26
  87.4 1.6 %shard_map.150 = (f32[64,2304]{1,0:T(8,128)S(1)}, bf16[64,2304]{1,0:T(8,128)(2,1)S(1)}) custom-call(bf16[128,1024]{1,0:T(8,128)(2,1)S(1)} %get-tuple-element.71.codes.codes_a, bf16[2304,1024]{1,0:T(8,128)(2,1)S(1)} %bitcast.15), custom_call_target="tpu_custom_call" | custom-call | flops 603979776 | bytes 4718592 | tf_op jit(solution)/shard_map/pallas_call | solution.py:418
  92.4 4.5 %collective-permute-done.29 = bf16[32,2304]{1,0:T(8,128)(2,1)S(1)} collective-permute-done((bf16[32,2304]{1,0:T(8,128)(2,1)S(1)}, bf16[32,2304]{1,0:T(8,128)(2,1)S(1)}, u32[]{:S(2)}, u32[]{:S(2)}) %collective-permute-start.29) | collective-permute-done | bytes 147488 | tf_op jit(solution)/shard_map/ppermute | solution.py:26
  98.2 2.0 %collective-permute-start.32 = (bf16[8,2304]{1,0:T(8,128)(2,1)S(1)}, bf16[8,2304]{1,0:T(8,128)(2,1)S(1)}, u32[]{:S(2)}, u32[]{:S(2)}) collective-permute-start(bf16[8,2304]{1,0:T(8,128)(2,1)S(1)} %get-tuple-element.109), channel_id=1, source_target_pairs={{0,3},{1,2},{2,1},{3,0},{4,7},{5,6},{6,5},{7,4},{8,11},{9,10},{10,... | collective-permute-start | bytes 110600 | tf_op jit(solution)/shard_map/ppermute | solution.py:26
  100.6 2.1 %collective-permute-start.25 = (bf16[8,2304]{1,0:T(8,128)(2,1)S(1)}, bf16[8,2304]{1,0:T(8,128)(2,1)S(1)}, u32[]{:S(2)}, u32[]{:S(2)}) collective-permute-start(bf16[8,2304]{1,0:T(8,128)(2,1)S(1)} %get-tuple-element.111), channel_id=1, source_target_pairs={{0,1},{1,0},{2,3},{3,2},{4,5},{5,4},{6,7},{7,6},{8,9},{9,8},{10,11... | collective-permute-start | bytes 110600 | tf_op jit(solution)/shard_map/ppermute | solution.py:26
  102.7 2.0 %collective-permute-start.27 = (bf16[8,2304]{1,0:T(8,128)(2,1)S(1)}, bf16[8,2304]{1,0:T(8,128)(2,1)S(1)}, u32[]{:S(2)}, u32[]{:S(2)}) collective-permute-start(bf16[8,2304]{1,0:T(8,128)(2,1)S(1)} %get-tuple-element.112), channel_id=1, source_target_pairs={{0,3},{1,2},{2,1},{3,0},{4,7},{5,6},{6,5},{7,4},{8,11},{9,10},{10,... | collective-permute-start | bytes 110600 | tf_op jit(solution)/shard_map/ppermute | solution.py:26
  105.1 1.9 %collective-permute-start.40 = (bf16[8,2304]{1,0:T(8,128)(2,1)S(1)}, bf16[8,2304]{1,0:T(8,128)(2,1)S(1)}, u32[]{:S(2)}, u32[]{:S(2)}) collective-permute-start(bf16[8,2304]{1,0:T(8,128)(2,1)S(1)} %fusion.14), channel_id=1, source_target_pairs={{0,3},{1,2},{2,1},{3,0},{4,7},{5,6},{6,5},{7,4},{8,11},{9,10},{10,... | collective-permute-start | bytes 110600 | tf_op jit(solution)/shard_map/ppermute | solution.py:26
  110.1 2.0 %collective-permute-start.35 = (bf16[8,2304]{1,0:T(8,128)(2,1)S(1)}, bf16[8,2304]{1,0:T(8,128)(2,1)S(1)}, u32[]{:S(2)}, u32[]{:S(2)}) collective-permute-start(bf16[8,2304]{1,0:T(8,128)(2,1)S(1)} %subtract_convert_fusion), channel_id=1, source_target_pairs={{0,3},{1,2},{2,1},{3,0},{4,7},{5,6},{6,5},{7,4},{8,11},{9,10},{10,... | collective-permute-start | bytes 110600 | tf_op jit(solution)/shard_map/ppermute | solution.py:26
  112.2 2.3 %collective-permute-start.33 = (bf16[8,2304]{1,0:T(8,128)(2,1)S(1)}, bf16[8,2304]{1,0:T(8,128)(2,1)S(1)}, u32[]{:S(2)}, u32[]{:S(2)}) collective-permute-start(bf16[8,2304]{1,0:T(8,128)(2,1)S(1)} %subtract_convert_fusion), channel_id=1, source_target_pairs={{0,1},{1,0},{2,3},{3,2},{4,5},{5,4},{6,7},{7,6},{8,9},{9,8},{10,11... | collective-permute-start | bytes 110600 | tf_op jit(solution)/shard_map/ppermute | solution.py:26
  114.6 1.6 %collective-permute-start.41 = (bf16[32,2304]{1,0:T(8,128)(2,1)S(1)}, bf16[32,2304]{1,0:T(8,128)(2,1)S(1)}, u32[]{:S(2)}, u32[]{:S(2)}) collective-permute-start(bf16[32,2304]{1,0:T(8,128)(2,1)S(1)} %pad_maximum_fusion.8._), channel_id=1, source_target_pairs={{0,8},{4,12},{8,0},{12,4},{1,9},{5,13},{9,1},{13,5},{2,10},{6,14},... | collective-permute-start | bytes 442376 | tf_op jit(solution)/shard_map/ppermute | solution.py:26
  120.0 2.3 %collective-permute-done.36 = bf16[32,2304]{1,0:T(8,128)(2,1)S(1)} collective-permute-done((bf16[32,2304]{1,0:T(8,128)(2,1)S(1)}, bf16[32,2304]{1,0:T(8,128)(2,1)S(1)}, u32[]{:S(2)}, u32[]{:S(2)}) %collective-permute-start.36) | collective-permute-done | bytes 147488 | tf_op jit(solution)/shard_map/ppermute | solution.py:26
  127.8 4.7 %collective-permute-done.43 = bf16[128,1024]{1,0:T(8,128)(2,1)S(1)} collective-permute-done((bf16[128,1024]{1,0:T(8,128)(2,1)S(1)}, bf16[128,1024]{1,0:T(8,128)(2,1)S(1)}, u32[]{:S(2)}, u32[]{:S(2)}) %collective-permute-start.43) | collective-permute-done | bytes 262176 | tf_op jit(solution)/shard_map/ppermute | solution.py:26
  132.6 5.0 %collective-permute-done.44 = bf16[128,1024]{1,0:T(8,128)(2,1)S(1)} collective-permute-done((bf16[128,1024]{1,0:T(8,128)(2,1)S(1)}, bf16[128,1024]{1,0:T(8,128)(2,1)S(1)}, u32[]{:S(2)}, u32[]{:S(2)}) %collective-permute-start.44) | collective-permute-done | bytes 262176 | tf_op jit(solution)/shard_map/ppermute | solution.py:26
  137.7 3.1 %shard_map.154 = (bf16[2304,1024]{1,0:T(8,128)(2,1)}, f32[1,1024]{1,0:T(1,128)}) custom-call(f32[2304,1024]{1,0:T(8,128)S(1)} %get-tuple-element.80.total, bf16[2304,256]{1,0:T(8,128)(2,1)S(1)} %get-tuple-element.81.turned, bf16[128,1024]{1,0:T(8,128)(2,1)S(1)} %multiply_convert_fusion.1.grad_a, bf16[128,1024]{1,0:T(8,128)(2,1)S(1)} %multiply_convert_fusion.grad_b), custom_call_target="tpu_custom_call" | custom-call | flops 1207959552 | bytes 14155776 | tf_op jit(solution)/shard_map/pallas_call | solution.py:489
  (151 shorter events, 44.2 us)
Async XLA Ops:
  0.6 8.8 %collective-permute-start.2 = (bf16[1,288,128]{2,1,0:T(8,128)(2,1)}, bf16[1,288,128]{2,1,0:T(8,128)(2,1)S(1)}, u32[]{:S(2)}, u32[]{:S(2)}) collective-permute-start(bf16[1,288,128]{2,1,0:T(8,128)(2,1)} %bitcast.16), channel_id=1, source_target_pairs={{0,3},{1,2},{2,1},{3,0},{4,7},{5,6},{6,5},{7,4},{8,11},{9,10},{10,... | collective-permute-start | bytes 221192 | tf_op jit(solution)/shard_map/ppermute | solution.py:26
  5.8 6.4 %collective-permute-start.1 = (bf16[1,288,128]{2,1,0:T(8,128)(2,1)}, bf16[1,288,128]{2,1,0:T(8,128)(2,1)S(1)}, u32[]{:S(2)}, u32[]{:S(2)}) collective-permute-start(bf16[1,288,128]{2,1,0:T(8,128)(2,1)} %bitcast.17), channel_id=1, source_target_pairs={{0,2},{1,3},{2,0},{3,1},{4,6},{5,7},{6,4},{7,5},{8,10},{9,11},{10,... | collective-permute-start | bytes 221192 | tf_op jit(solution)/shard_map/ppermute | solution.py:26
  5.8 6.4 %collective-permute-start = (bf16[1,288,128]{2,1,0:T(8,128)(2,1)}, bf16[1,288,128]{2,1,0:T(8,128)(2,1)S(1)}, u32[]{:S(2)}, u32[]{:S(2)}) collective-permute-start(bf16[1,288,128]{2,1,0:T(8,128)(2,1)} %bitcast.18), channel_id=1, source_target_pairs={{0,1},{1,0},{2,3},{3,2},{4,5},{5,4},{6,7},{7,6},{8,9},{9,8},{10,11... | collective-permute-start | bytes 221192 | tf_op jit(solution)/shard_map/ppermute | solution.py:26
  13.1 8.4 %collective-permute-start.3 = (bf16[4,288,128]{2,1,0:T(8,128)(2,1)S(1)}, bf16[4,288,128]{2,1,0:T(8,128)(2,1)S(1)}, u32[]{:S(2)}, u32[]{:S(2)}) collective-permute-start(bf16[4,288,128]{2,1,0:T(8,128)(2,1)S(1)} %pad_maximum_fusion.2), channel_id=1, source_target_pairs={{0,8},{4,12},{8,0},{12,4},{1,9},{5,13},{9,1},{13,5},{2,10},{6,14},... | collective-permute-start | bytes 884744 | tf_op jit(solution)/shard_map/ppermute | solution.py:26
  31.6 9.1 %collective-permute-start.6 = (bf16[32,4608]{1,0:T(8,128)(2,1)S(1)}, bf16[32,4608]{1,0:T(8,128)(2,1)S(1)}, u32[]{:S(2)}, u32[]{:S(2)}) collective-permute-start(bf16[32,4608]{1,0:T(8,128)(2,1)S(1)} %slice.156), channel_id=1, source_target_pairs={{0,8},{4,12},{8,0},{12,4},{1,9},{5,13},{9,1},{13,5},{2,10},{6,14},... | collective-permute-start | bytes 884744 | tf_op jit(solution)/shard_map/ppermute | solution.py:26
  40.8 5.4 %collective-permute-start.7 = (bf16[8,4608]{1,0:T(8,128)(2,1)S(1)}, bf16[8,4608]{1,0:T(8,128)(2,1)S(1)}, u32[]{:S(2)}, u32[]{:S(2)}) collective-permute-start(bf16[8,4608]{1,0:T(8,128)(2,1)S(1)} %get-tuple-element.103), channel_id=1, source_target_pairs={{0,1},{1,0},{2,3},{3,2},{4,5},{5,4},{6,7},{7,6},{8,9},{9,8},{10,11... | collective-permute-start | bytes 221192 | tf_op jit(solution)/shard_map/ppermute | solution.py:26
  41.2 6.3 %collective-permute-start.9 = (bf16[8,4608]{1,0:T(8,128)(2,1)S(1)}, bf16[8,4608]{1,0:T(8,128)(2,1)S(1)}, u32[]{:S(2)}, u32[]{:S(2)}) collective-permute-start(bf16[8,4608]{1,0:T(8,128)(2,1)S(1)} %get-tuple-element.104), channel_id=1, source_target_pairs={{0,3},{1,2},{2,1},{3,0},{4,7},{5,6},{6,5},{7,4},{8,11},{9,10},{10,... | collective-permute-start | bytes 221192 | tf_op jit(solution)/shard_map/ppermute | solution.py:26
  42.8 7.7 %collective-permute-start.8 = (bf16[8,4608]{1,0:T(8,128)(2,1)S(1)}, bf16[8,4608]{1,0:T(8,128)(2,1)S(1)}, u32[]{:S(2)}, u32[]{:S(2)}) collective-permute-start(bf16[8,4608]{1,0:T(8,128)(2,1)S(1)} %get-tuple-element.105), channel_id=1, source_target_pairs={{0,2},{1,3},{2,0},{3,1},{4,6},{5,7},{6,4},{7,5},{8,10},{9,11},{10,... | collective-permute-start | bytes 221192 | tf_op jit(solution)/shard_map/ppermute | solution.py:26
  50.8 6.0 %collective-permute-start.12 = (bf16[8,2304]{1,0:T(8,128)(2,1)S(1)}, bf16[8,2304]{1,0:T(8,128)(2,1)S(1)}, u32[]{:S(2)}, u32[]{:S(2)}) collective-permute-start(bf16[8,2304]{1,0:T(8,128)(2,1)S(1)} %get-tuple-element.117), channel_id=1, source_target_pairs={{0,3},{1,2},{2,1},{3,0},{4,7},{5,6},{6,5},{7,4},{8,11},{9,10},{10,... | collective-permute-start | bytes 110600 | tf_op jit(solution)/shard_map/ppermute | solution.py:26
  57.6 10.1 %collective-permute-start.13 = (bf16[32,2304]{1,0:T(8,128)(2,1)S(1)}, bf16[32,2304]{1,0:T(8,128)(2,1)S(1)}, u32[]{:S(2)}, u32[]{:S(2)}) collective-permute-start(bf16[32,2304]{1,0:T(8,128)(2,1)S(1)} %pad_maximum_fusion.5._), channel_id=1, source_target_pairs={{0,8},{4,12},{8,0},{12,4},{1,9},{5,13},{9,1},{13,5},{2,10},{6,14},... | collective-permute-start | bytes 442376 | tf_op jit(solution)/shard_map/ppermute | solution.py:26
  59.3 5.8 %collective-permute-start.18 = (bf16[8,2304]{1,0:T(8,128)(2,1)S(1)}, bf16[8,2304]{1,0:T(8,128)(2,1)S(1)}, u32[]{:S(2)}, u32[]{:S(2)}) collective-permute-start(bf16[8,2304]{1,0:T(8,128)(2,1)S(1)} %collective-permute-done.15), channel_id=1, source_target_pairs={{0,3},{1,2},{2,1},{3,0},{4,7},{5,6},{6,5},{7,4},{8,11},{9,10},{10,... | collective-permute-start | bytes 110600 | tf_op jit(solution)/shard_map/ppermute | solution.py:26
  61.3 5.3 %collective-permute-start.17 = (bf16[8,2304]{1,0:T(8,128)(2,1)S(1)}, bf16[8,2304]{1,0:T(8,128)(2,1)S(1)}, u32[]{:S(2)}, u32[]{:S(2)}) collective-permute-start(bf16[8,2304]{1,0:T(8,128)(2,1)S(1)} %collective-permute-done.15), channel_id=1, source_target_pairs={{0,2},{1,3},{2,0},{3,1},{4,6},{5,7},{6,4},{7,5},{8,10},{9,11},{10,... | collective-permute-start | bytes 110600 | tf_op jit(solution)/shard_map/ppermute | solution.py:26
  66.6 5.2 %collective-permute-start.19 = (bf16[32,2304]{1,0:T(8,128)(2,1)S(1)}, bf16[32,2304]{1,0:T(8,128)(2,1)S(1)}, u32[]{:S(2)}, u32[]{:S(2)}) collective-permute-start(bf16[32,2304]{1,0:T(8,128)(2,1)S(1)} %pad_maximum_fusion.6), channel_id=1, source_target_pairs={{0,8},{4,12},{8,0},{12,4},{1,9},{5,13},{9,1},{13,5},{2,10},{6,14},... | collective-permute-start | bytes 442376 | tf_op jit(solution)/shard_map/ppermute | solution.py:26
  72.8 9.2 %collective-permute-start.21 = (bf16[128,1024]{1,0:T(8,128)(2,1)S(1)}, bf16[128,1024]{1,0:T(8,128)(2,1)S(1)}, u32[]{:S(2)}, u32[]{:S(2)}) collective-permute-start(bf16[128,1024]{1,0:T(8,128)(2,1)S(1)} %get-tuple-element.67), channel_id=1, source_target_pairs={{0,16},{16,0},{1,17},{17,1},{2,18},{18,2},{3,19},{19,3},{4,20},{20... | collective-permute-start | bytes 786440 | tf_op jit(solution)/shard_map/ppermute | solution.py:26
  75.2 11.9 %collective-permute-start.22 = (bf16[128,1024]{1,0:T(8,128)(2,1)S(1)}, bf16[128,1024]{1,0:T(8,128)(2,1)S(1)}, u32[]{:S(2)}, u32[]{:S(2)}) collective-permute-start(bf16[128,1024]{1,0:T(8,128)(2,1)S(1)} %get-tuple-element.69), channel_id=1, source_target_pairs={{0,16},{16,0},{1,17},{17,1},{2,18},{18,2},{3,19},{19,3},{4,20},{20... | collective-permute-start | bytes 786440 | tf_op jit(solution)/shard_map/ppermute | solution.py:26
  83.9 6.1 %collective-permute-start.28 = (bf16[64,2304]{1,0:T(8,128)(2,1)S(1)}, bf16[64,2304]{1,0:T(8,128)(2,1)S(1)}, u32[]{:S(2)}, u32[]{:S(2)}) collective-permute-start(bf16[64,2304]{1,0:T(8,128)(2,1)S(1)} %get-tuple-element.75), channel_id=1, source_target_pairs={{0,4},{4,0},{8,12},{12,8},{1,5},{5,1},{9,13},{13,9},{2,6},{6,2},{1... | collective-permute-start | bytes 884744 | tf_op jit(solution)/shard_map/ppermute | solution.py:26
  90.2 6.8 %collective-permute-start.29 = (bf16[32,2304]{1,0:T(8,128)(2,1)S(1)}, bf16[32,2304]{1,0:T(8,128)(2,1)S(1)}, u32[]{:S(2)}, u32[]{:S(2)}) collective-permute-start(bf16[32,2304]{1,0:T(8,128)(2,1)S(1)} %slice.157), channel_id=1, source_target_pairs={{0,8},{4,12},{8,0},{12,4},{1,9},{5,13},{9,1},{13,5},{2,10},{6,14},... | collective-permute-start | bytes 442376 | tf_op jit(solution)/shard_map/ppermute | solution.py:26
  91.3 9.2 %collective-permute-start.24 = (bf16[32,2304]{1,0:T(8,128)(2,1)S(1)}, bf16[32,2304]{1,0:T(8,128)(2,1)S(1)}, u32[]{:S(2)}, u32[]{:S(2)}) collective-permute-start(bf16[32,2304]{1,0:T(8,128)(2,1)S(1)} %slice.158), channel_id=1, source_target_pairs={{0,8},{4,12},{8,0},{12,4},{1,9},{5,13},{9,1},{13,5},{2,10},{6,14},... | collective-permute-start | bytes 442376 | tf_op jit(solution)/shard_map/ppermute | solution.py:26
  97.0 7.6 %collective-permute-start.30 = (bf16[8,2304]{1,0:T(8,128)(2,1)S(1)}, bf16[8,2304]{1,0:T(8,128)(2,1)S(1)}, u32[]{:S(2)}, u32[]{:S(2)}) collective-permute-start(bf16[8,2304]{1,0:T(8,128)(2,1)S(1)} %get-tuple-element.108), channel_id=1, source_target_pairs={{0,1},{1,0},{2,3},{3,2},{4,5},{5,4},{6,7},{7,6},{8,9},{9,8},{10,11... | collective-permute-start | bytes 110600 | tf_op jit(solution)/shard_map/ppermute | solution.py:26
  98.2 6.5 %collective-permute-start.32 = (bf16[8,2304]{1,0:T(8,128)(2,1)S(1)}, bf16[8,2304]{1,0:T(8,128)(2,1)S(1)}, u32[]{:S(2)}, u32[]{:S(2)}) collective-permute-start(bf16[8,2304]{1,0:T(8,128)(2,1)S(1)} %get-tuple-element.109), channel_id=1, source_target_pairs={{0,3},{1,2},{2,1},{3,0},{4,7},{5,6},{6,5},{7,4},{8,11},{9,10},{10,... | collective-permute-start | bytes 110600 | tf_op jit(solution)/shard_map/ppermute | solution.py:26
  100.1 5.0 %collective-permute-start.31 = (bf16[8,2304]{1,0:T(8,128)(2,1)S(1)}, bf16[8,2304]{1,0:T(8,128)(2,1)S(1)}, u32[]{:S(2)}, u32[]{:S(2)}) collective-permute-start(bf16[8,2304]{1,0:T(8,128)(2,1)S(1)} %get-tuple-element.110), channel_id=1, source_target_pairs={{0,2},{1,3},{2,0},{3,1},{4,6},{5,7},{6,4},{7,5},{8,10},{9,11},{10,... | collective-permute-start | bytes 110600 | tf_op jit(solution)/shard_map/ppermute | solution.py:26
  100.6 8.0 %collective-permute-start.25 = (bf16[8,2304]{1,0:T(8,128)(2,1)S(1)}, bf16[8,2304]{1,0:T(8,128)(2,1)S(1)}, u32[]{:S(2)}, u32[]{:S(2)}) collective-permute-start(bf16[8,2304]{1,0:T(8,128)(2,1)S(1)} %get-tuple-element.111), channel_id=1, source_target_pairs={{0,1},{1,0},{2,3},{3,2},{4,5},{5,4},{6,7},{7,6},{8,9},{9,8},{10,11... | collective-permute-start | bytes 110600 | tf_op jit(solution)/shard_map/ppermute | solution.py:26
  102.7 6.9 %collective-permute-start.27 = (bf16[8,2304]{1,0:T(8,128)(2,1)S(1)}, bf16[8,2304]{1,0:T(8,128)(2,1)S(1)}, u32[]{:S(2)}, u32[]{:S(2)}) collective-permute-start(bf16[8,2304]{1,0:T(8,128)(2,1)S(1)} %get-tuple-element.112), channel_id=1, source_target_pairs={{0,3},{1,2},{2,1},{3,0},{4,7},{5,6},{6,5},{7,4},{8,11},{9,10},{10,... | collective-permute-start | bytes 110600 | tf_op jit(solution)/shard_map/ppermute | solution.py:26
  104.7 5.4 %collective-permute-start.26 = (bf16[8,2304]{1,0:T(8,128)(2,1)S(1)}, bf16[8,2304]{1,0:T(8,128)(2,1)S(1)}, u32[]{:S(2)}, u32[]{:S(2)}) collective-permute-start(bf16[8,2304]{1,0:T(8,128)(2,1)S(1)} %get-tuple-element.113), channel_id=1, source_target_pairs={{0,2},{1,3},{2,0},{3,1},{4,6},{5,7},{6,4},{7,5},{8,10},{9,11},{10,... | collective-permute-start | bytes 110600 | tf_op jit(solution)/shard_map/ppermute | solution.py:26
  105.1 7.1 %collective-permute-start.40 = (bf16[8,2304]{1,0:T(8,128)(2,1)S(1)}, bf16[8,2304]{1,0:T(8,128)(2,1)S(1)}, u32[]{:S(2)}, u32[]{:S(2)}) collective-permute-start(bf16[8,2304]{1,0:T(8,128)(2,1)S(1)} %fusion.14), channel_id=1, source_target_pairs={{0,3},{1,2},{2,1},{3,0},{4,7},{5,6},{6,5},{7,4},{8,11},{9,10},{10,... | collective-permute-start | bytes 110600 | tf_op jit(solution)/shard_map/ppermute | solution.py:26
  107.1 7.5 %collective-permute-start.39 = (bf16[8,2304]{1,0:T(8,128)(2,1)S(1)}, bf16[8,2304]{1,0:T(8,128)(2,1)S(1)}, u32[]{:S(2)}, u32[]{:S(2)}) collective-permute-start(bf16[8,2304]{1,0:T(8,128)(2,1)S(1)} %fusion.14), channel_id=1, source_target_pairs={{0,2},{1,3},{2,0},{3,1},{4,6},{5,7},{6,4},{7,5},{8,10},{9,11},{10,... | collective-permute-start | bytes 110600 | tf_op jit(solution)/shard_map/ppermute | solution.py:26
  108.6 6.0 %collective-permute-start.38 = (bf16[8,2304]{1,0:T(8,128)(2,1)S(1)}, bf16[8,2304]{1,0:T(8,128)(2,1)S(1)}, u32[]{:S(2)}, u32[]{:S(2)}) collective-permute-start(bf16[8,2304]{1,0:T(8,128)(2,1)S(1)} %fusion.14), channel_id=1, source_target_pairs={{0,1},{1,0},{2,3},{3,2},{4,5},{5,4},{6,7},{7,6},{8,9},{9,8},{10,11... | collective-permute-start | bytes 110600 | tf_op jit(solution)/shard_map/ppermute | solution.py:26
  110.1 6.6 %collective-permute-start.35 = (bf16[8,2304]{1,0:T(8,128)(2,1)S(1)}, bf16[8,2304]{1,0:T(8,128)(2,1)S(1)}, u32[]{:S(2)}, u32[]{:S(2)}) collective-permute-start(bf16[8,2304]{1,0:T(8,128)(2,1)S(1)} %subtract_convert_fusion), channel_id=1, source_target_pairs={{0,3},{1,2},{2,1},{3,0},{4,7},{5,6},{6,5},{7,4},{8,11},{9,10},{10,... | collective-permute-start | bytes 110600 | tf_op jit(solution)/shard_map/ppermute | solution.py:26
  114.6 5.2 %collective-permute-start.41 = (bf16[32,2304]{1,0:T(8,128)(2,1)S(1)}, bf16[32,2304]{1,0:T(8,128)(2,1)S(1)}, u32[]{:S(2)}, u32[]{:S(2)}) collective-permute-start(bf16[32,2304]{1,0:T(8,128)(2,1)S(1)} %pad_maximum_fusion.8._), channel_id=1, source_target_pairs={{0,8},{4,12},{8,0},{12,4},{1,9},{5,13},{9,1},{13,5},{2,10},{6,14},... | collective-permute-start | bytes 442376 | tf_op jit(solution)/shard_map/ppermute | solution.py:26
  117.0 5.2 %collective-permute-start.36 = (bf16[32,2304]{1,0:T(8,128)(2,1)S(1)}, bf16[32,2304]{1,0:T(8,128)(2,1)S(1)}, u32[]{:S(2)}, u32[]{:S(2)}) collective-permute-start(bf16[32,2304]{1,0:T(8,128)(2,1)S(1)} %pad_maximum_fusion.7), channel_id=1, source_target_pairs={{0,8},{4,12},{8,0},{12,4},{1,9},{5,13},{9,1},{13,5},{2,10},{6,14},... | collective-permute-start | bytes 442376 | tf_op jit(solution)/shard_map/ppermute | solution.py:26
  123.2 9.2 %collective-permute-start.43 = (bf16[128,1024]{1,0:T(8,128)(2,1)S(1)}, bf16[128,1024]{1,0:T(8,128)(2,1)S(1)}, u32[]{:S(2)}, u32[]{:S(2)}) collective-permute-start(bf16[128,1024]{1,0:T(8,128)(2,1)S(1)} %get-tuple-element.84), channel_id=1, source_target_pairs={{0,16},{16,0},{1,17},{17,1},{2,18},{18,2},{3,19},{19,3},{4,20},{20... | collective-permute-start | bytes 786440 | tf_op jit(solution)/shard_map/ppermute | solution.py:26
  125.6 12.0 %collective-permute-start.44 = (bf16[128,1024]{1,0:T(8,128)(2,1)S(1)}, bf16[128,1024]{1,0:T(8,128)(2,1)S(1)}, u32[]{:S(2)}, u32[]{:S(2)}) collective-permute-start(bf16[128,1024]{1,0:T(8,128)(2,1)S(1)} %get-tuple-element.87), channel_id=1, source_target_pairs={{0,16},{16,0},{1,17},{17,1},{2,18},{18,2},{3,19},{19,3},{4,20},{20... | collective-permute-start | bytes 786440 | tf_op jit(solution)/shard_map/ppermute | solution.py:26
  (22 other events, 181.8 us)
